TPU v7x, 128 devices: a whole 4x4x4 slice. The times are simulated.
128 devices in a mesh: tm: 16 (over x, y), bl: 8 (over z, core).
Axes of the slice: x: 4, y: 4, z: 4, core: 2. Of those that a mesh axis runs over, the one named last changes fastest.
Arguments:
- visibilities: bfloat16 [65536, 2, 240], P(('tm', 'bl')), may hold values from -12 to 12
- noise_weight: float32 [65536], P(('tm', 'bl')), may hold values from 0.005 to 0.05
- keep_flag: int32 [65536], P(('tm', 'bl')), may hold values 0 or 1
- station_pairs: int32 [2, 65536], P(None, ('tm', 'bl')), may hold values from 0 to 63, as said below
- tile_owner: int32 [65536, 1], P(('tm', 'bl')), may hold values from 0 to 127; in each aligned block of 512 rows (0 to 511, 512 to 1023, ...) at most 8 rows name the same one
- tile_offset: int32 [65536], P(('tm', 'bl')), may hold values from 0 to 32760
- kernel_taps: float32 [8, 65536], P(None, ('tm', 'bl')), may hold values from 0.1 to 1
- gain_field: float32 [16, 64, 8, 2, 240], P('tm', 'bl'), may hold values from 0.25 to 1.75
- sky_grid: float32 [2, 8, 2, 4194304], P(None, None, None, ('tm', 'bl')), may hold values from -4 to 4
Outputs:
- gain_gradient: float32 [16, 64, 8, 2, 240], P('tm', 'bl')
- grid_gradient: float32 [2, 8, 2, 4194304], P(None, None, None, ('tm', 'bl'))
Inputs may be any that keep to these rules, and one draw needn't show every extreme that they name: `station_pairs`: the two stations of a row differ. `tile_owner`: among the rows of one device no value appears more than 8 times, and in some device one appears exactly 8 times.
All inputs are finite; a program needn't handle non-finite values. No bound on the sum of `keep_flag` on one device may be relied on, other than what follows from the above.
Results may differ from a plain program's by a relative error of at most 0.0003.
Values sent between devices are 32-bit elements; how exact they have to be, the bound alone decides.
A program may use at most 128 MiB of HBM per device.

v0:
```python
import jax
import jax.numpy as jnp
from jax import lax
from jax.sharding import PartitionSpec as P

smoothness = 4.0


def spectral_table(channels, spectral_terms):
    channel_ramp = 2.0 * jnp.arange(channels, dtype=jnp.float32) / (channels - 1) - 1.0
    powers = jnp.arange(spectral_terms, dtype=jnp.float32)
    return channel_ramp[None, :] ** powers[:, None]


def complex_mul(x_re, x_im, y_re, y_im):
    return (x_re * y_re - x_im * y_im, x_re * y_im + x_im * y_re)


def row_grads(visibilities, noise_weight, keep_flag, station_pairs, gains_all, degrid):
    row_count = visibilities.shape[0]
    stations = gains_all.shape[0]
    facets = gains_all.shape[1]
    channels = gains_all.shape[3]
    spectral_terms = degrid.shape[2]
    spectrum = spectral_table(channels, spectral_terms)
    first_station = station_pairs[0]
    second_station = station_pairs[1]
    observed = visibilities.astype(jnp.float32)
    scaling = (noise_weight * keep_flag.astype(jnp.float32))[:, None, None]
    onehot_first = (
        jnp.arange(stations, dtype=jnp.int32)[:, None] == first_station[None, :]
    ).astype(jnp.float32)
    onehot_second = (
        jnp.arange(stations, dtype=jnp.int32)[:, None] == second_station[None, :]
    ).astype(jnp.float32)

    def facet_parts(facet_index):
        gain_slab = lax.dynamic_index_in_dim(gains_all, facet_index, 1, keepdims=False)
        left_gain = jnp.take(gain_slab, first_station, axis=0)
        right_gain = jnp.take(gain_slab, second_station, axis=0)
        degrid_slab = lax.dynamic_index_in_dim(degrid, facet_index, 1, keepdims=False)
        facet_model = jnp.einsum(
            "xtr,tc->xrc", degrid_slab, spectrum, precision=lax.Precision.HIGHEST
        )
        return (left_gain, right_gain, facet_model)

    def add_model(facet_index, running):
        left_gain, right_gain, facet_model = facet_parts(facet_index)
        pair_re, pair_im = complex_mul(
            left_gain[:, 0], left_gain[:, 1], right_gain[:, 0], -right_gain[:, 1]
        )
        vis_re, vis_im = complex_mul(pair_re, pair_im, facet_model[0], facet_model[1])
        return running + jnp.stack([vis_re, vis_im], axis=1)

    predicted = lax.fori_loop(
        0, facets, add_model, jnp.zeros((row_count, 2, channels), jnp.float32)
    )
    error = scaling * (observed - predicted)
    err_re = error[:, 0]
    err_im = error[:, 1]

    def add_grads(facet_index, accums):
        gain_acc, degrid_acc = accums
        left_gain, right_gain, facet_model = facet_parts(facet_index)
        left_re, left_im = (left_gain[:, 0], left_gain[:, 1])
        right_re, right_im = (right_gain[:, 0], right_gain[:, 1])
        model_re, model_im = (facet_model[0], facet_model[1])
        first_re, first_im = complex_mul(err_re, err_im, right_re, right_im)
        grad_are, grad_aim = complex_mul(first_re, first_im, model_re, -model_im)
        second_re, second_im = complex_mul(err_re, -err_im, left_re, left_im)
        grad_bre, grad_bim = complex_mul(second_re, second_im, model_re, model_im)
        third_re, third_im = complex_mul(err_re, err_im, left_re, -left_im)
        grad_mre, grad_mim = complex_mul(third_re, third_im, right_re, right_im)
        grad_left = -jnp.stack([grad_are, grad_aim], axis=1).reshape(row_count, 2 * channels)
        grad_right = -jnp.stack([grad_bre, grad_bim], axis=1).reshape(row_count, 2 * channels)
        per_station = jnp.dot(onehot_first, grad_left, precision=lax.Precision.HIGHEST)
        per_station = per_station + jnp.dot(
            onehot_second, grad_right, precision=lax.Precision.HIGHEST
        )
        gain_acc = lax.dynamic_update_index_in_dim(
            gain_acc, per_station.reshape(stations, 2, channels), facet_index, 1
        )
        grad_model = -jnp.stack([grad_mre, grad_mim], axis=0)
        grad_degrid = jnp.einsum(
            "xrc,tc->xtr", grad_model, spectrum, precision=lax.Precision.HIGHEST
        )
        degrid_acc = lax.dynamic_update_index_in_dim(degrid_acc, grad_degrid, facet_index, 1)
        return (gain_acc, degrid_acc)

    initial = (
        jnp.zeros((stations, facets, 2, channels), jnp.float32),
        jnp.zeros((2, facets, spectral_terms, row_count), jnp.float32),
    )
    return lax.fori_loop(0, facets, add_grads, initial)


def smooth_grad(gain_block):
    step_diff = gain_block[1:] - gain_block[:-1]
    from_below = jnp.pad(step_diff, ((1, 0), (0, 0), (0, 0), (0, 0), (0, 0)))
    from_above = jnp.pad(step_diff, ((0, 1), (0, 0), (0, 0), (0, 0), (0, 0)))
    return smoothness * (from_below - from_above)


def body(
    visibilities,
    noise_weight,
    keep_flag,
    station_pairs,
    tile_owner,
    tile_offset,
    kernel_taps,
    gain_field,
    sky_grid,
):
    row_count = visibilities.shape[0]
    taps_count = kernel_taps.shape[0]
    time_count = lax.axis_size("tm")
    group_count = lax.axis_size("bl")
    device_count = time_count * group_count
    capacity = max(2, 2 * row_count // device_count)
    slot_count = device_count * capacity
    grid_cells = sky_grid.shape[3]
    grid_planes = sky_grid.shape[0] * sky_grid.shape[1] * sky_grid.shape[2]
    row_owner = tile_owner[:, 0]
    owner_hits = (row_owner[:, None] == jnp.arange(device_count, dtype=jnp.int32)[None, :]).astype(
        jnp.int32
    )
    earlier_hits = jnp.cumsum(owner_hits, axis=0) - owner_hits
    slot_rank = jnp.sum(earlier_hits * owner_hits, axis=1)
    slot_index = row_owner * capacity + slot_rank
    send_offsets = jnp.zeros((slot_count,), jnp.int32).at[slot_index].set(tile_offset)
    send_taps = jnp.zeros((slot_count, taps_count), jnp.float32).at[slot_index].set(kernel_taps.T)
    got_offsets, got_taps = (
        lax.all_to_all(send_offsets, ("tm", "bl"), split_axis=0, concat_axis=0, tiled=True),
        lax.all_to_all(send_taps, ("tm", "bl"), split_axis=0, concat_axis=0, tiled=True),
    )
    grid_flat = sky_grid.reshape(grid_planes, grid_cells)
    cell_index = got_offsets[:, None] + jnp.arange(taps_count, dtype=jnp.int32)[None, :]
    tile_values = jnp.sum(grid_flat[:, cell_index] * got_taps[None], axis=2)
    returned = lax.all_to_all(tile_values, ("tm", "bl"), split_axis=1, concat_axis=1, tiled=True)
    degrid = returned[:, slot_index].reshape(
        sky_grid.shape[0], sky_grid.shape[1], sky_grid.shape[2], row_count
    )
    all_gains = lax.all_gather(gain_field, "bl", axis=1, tiled=True)
    data_gains, grad_degrid = row_grads(
        visibilities, noise_weight, keep_flag, station_pairs, all_gains[0], degrid
    )
    summed_gains = lax.psum(data_gains, "bl")
    owned_count = gain_field.shape[1]
    owned_part = lax.dynamic_slice_in_dim(
        summed_gains, lax.axis_index("bl") * owned_count, owned_count, 0
    )[None]
    by_station = lax.all_to_all(gain_field, "tm", split_axis=4, concat_axis=0, tiled=True)
    prior_block = smooth_grad(by_station)
    prior_here = lax.all_to_all(prior_block, "tm", split_axis=0, concat_axis=4, tiled=True)
    gain_gradient = owned_part + prior_here
    send_grad = (
        jnp.zeros((grid_planes, slot_count), jnp.float32)
        .at[:, slot_index]
        .set(grad_degrid.reshape(grid_planes, row_count))
    )
    got_grad = lax.all_to_all(send_grad, ("tm", "bl"), split_axis=1, concat_axis=1, tiled=True)
    local_grid = (
        jnp.zeros((grid_planes, grid_cells), jnp.float32)
        .at[:, cell_index]
        .add(got_grad[:, :, None] * got_taps[None])
    )
    grid_gradient = local_grid.reshape(sky_grid.shape)
    return (gain_gradient, grid_gradient)


def solution(mesh):
    return jax.shard_map(
        body,
        mesh=mesh,
        in_specs=(
            P(("tm", "bl"), None, None),
            P(("tm", "bl")),
            P(("tm", "bl")),
            P(None, ("tm", "bl")),
            P(("tm", "bl"), None),
            P(("tm", "bl")),
            P(None, ("tm", "bl")),
            P("tm", "bl", None, None, None),
            P(None, None, None, ("tm", "bl")),
        ),
        out_specs=(P("tm", "bl", None, None, None), P(None, None, None, ("tm", "bl"))),
        check_vma=False,
    )
```

profile of v0, /device:TPU:1, one launch (start us, length us, event | category | flops | bytes accessed | tf_op | source)
XLA Modules:
  0.0 506.9 jit_solution(759661604377419789)
XLA Ops:
  9.9 2.6 scatter_custom_fusion
  13.2 11.5 %all-to-all-start = ((s32[128,8,1]{1,2,0:T(1,128)}), s32[128,8,1]{1,2,0:T(1,128)S(1)}, u32[]{:S(2)}, u32[]{:S(2)}) async-start(s32[128,8,1]{1,2,0:T(1,128)} %bitcast.10), calls=%async_computation | async-start | bytes 131072 | tf_op jit(solution)/shard_map/all_to_all | solution.py:134
  26.4 16.0 %all_gather.3 = f32[1,64,8,2,240]{4,3,1,2,0:T(2,128)} all-gather(f32[1,8,8,2,240]{4,3,1,2,0:T(2,128)S(1)} %copy.62), channel_id=1, replica_groups=mesh['tm'=16,'bl'=8] {'bl'}, dimensions={1}, use_global_device_ids=true | all-gather | bytes 1105920 | tf_op jit(solution)/shard_map/all_gather | solution.py:144
  45.1 6.0 %reshape.393 = f32[32,32768]{1,0:T(8,128)} reshape(f32[2,8,2,32768]{3,2,1,0:T(2,128)} %param.23) | data formatting | bytes 8388608 | tf_op jit(solution)/shard_map/reshape | solution.py:137
  51.2 10.4 %copy.66 = f32[32,32768]{0,1:T(8,128)} copy(f32[32,32768]{1,0:T(8,128)} %reshape.393) | data formatting | bytes 8388608 | tf_op jit(solution)/shard_map/reshape | solution.py:137
  65.8 8.5 %all-to-all-start.1 = ((f32[128,8,8]{2,1,0:T(8,128)}), f32[128,8,8]{2,1,0:T(8,128)S(1)}, u32[]{:S(2)}, u32[]{:S(2)}) async-start(f32[128,8,8]{2,1,0:T(8,128)} %bitcast.13), calls=%async_computation.1 | async-start | bytes 1048576 | tf_op jit(solution)/shard_map/all_to_all | solution.py:135
  76.2 33.7 %gather_fusion.4 = f32[8192,32]{1,0:T(8,128)} fusion(f32[32,32768]{0,1:T(8,128)} %copy.66, s32[8192]{0:T(1024)S(1)} %broadcast_clamp_fusion), kind=kCustom, calls=%fused_computation.4 | custom fusion | bytes 2129920 | tf_op jit(solution)/shard_map/gather | solution.py:139
  110.0 7.2 %all-to-all-start.3 = ((f32[16,1,1920]{2,1,0:T(1,128)}), f32[16,1,1920]{2,1,0:T(1,128)S(1)}, u32[]{:S(2)}, u32[]{:S(2)}) async-start(f32[16,1,1920]{2,1,0:T(1,128)} %reshape.523), calls=%async_computation.3 | async-start | bytes 245760 | tf_op jit(solution)/shard_map/all_to_all | solution.py:153
  117.1 7.1 %fusion.45 = f32[1024,32]{1,0:T(8,128)S(1)} fusion(f32[8192,32]{1,0:T(8,128)} %gather_fusion.4, f32[1024,8]{1,0:T(8,128)S(1)} %bitcast.268), kind=kLoop, calls=%fused_computation.106 | loop fusion | flops 491520 | bytes 1212416 | tf_op jit(solution)/shard_map/reduce_sum | solution.py:139
  125.2 10.4 %all-to-all-start.2 = ((f32[128,1,256]{2,1,0:T(1,128)}), f32[128,1,256]{2,1,0:T(1,128)S(1)}, u32[]{:S(2)}, u32[]{:S(2)}) async-start(f32[128,1,256]{2,1,0:T(1,128)} %reshape.527), calls=%async_computation.2 | async-start | bytes 262144 | tf_op jit(solution)/shard_map/all_to_all | solution.py:140
  142.1 3.2 all-to-all-done.2
  145.3 4.2 all-to-all-start.4
  151.9 82.3 %while.34 = (s32[]{:T(128)}, f32[512,2,240]{0,2,1:T(8,128)}, f32[64,8,2,240]{3,2,0,1:T(2,128)}, s32[512]{0:T(512)S(1)}, s32[512]{0:T(512)S(1)}, /*index=5*/f32[2...) while((s32[]{:T(128)}, f32[512,2,240]{0,2,1:T(8,128)}, ...), condition=%wide.region_7.9_spmd.clone, body=%wide.region_6.8_spmd.clone.sunk | while | flops 8735747 | bytes 30760100 | solution.py:55
  152.9 2.6 gather_fusion
  156.1 2.6 gather_fusion.1
  183.8 2.6 gather_fusion
  236.9 166.3 %while.35 = (s32[]{:T(128)}, f32[64,8,2,240]{3,1,2,0:T(8,128)}, f32[2,8,2,512]{3,2,1,0:T(2,128)}, f32[512,240]{0,1:T(8,128)}, f32[64,8,2,240]{3,2,0,1:T(2,128)},...) while((s32[]{:T(128)}, f32[64,8,2,240]{3,1,2,0:T(8,128)}, ...), condition=%wide.region_9.11_spmd.clone.clone.clone, body=%wide.region_8.10_spmd.clone.clone.clone.sunk | while | flops 396215296 | bytes 45429904 | solution.py:94
  253.8 4.0 dynamic_update_slice.30
  274.6 4.0 dynamic_update_slice.30
  295.4 4.0 dynamic_update_slice.30
  300.4 2.6 gather_fusion.3
  316.1 4.0 dynamic_update_slice.30
  336.9 4.0 dynamic_update_slice.30
  345.7 2.6 gather_fusion.2
  357.7 4.0 dynamic_update_slice.30
  378.4 4.0 dynamic_update_slice.30
  399.2 4.0 dynamic_update_slice.30
  407.2 9.9 %all-to-all-start.5 = ((f32[128,1,256]{2,1,0:T(1,128)}), f32[128,1,256]{2,1,0:T(1,128)S(1)}, u32[]{:S(2)}, u32[]{:S(2)}) async-start(f32[128,1,256]{2,1,0:T(1,128)} %reshape.529), calls=%async_computation.5 | async-start | bytes 262144 | tf_op jit(solution)/shard_map/all_to_all | solution.py:162
  421.2 5.7 %all-to-all-done.5 = f32[128,1,256]{2,1,0:T(1,128)S(1)} async-done(((f32[128,1,256]{2,1,0:T(1,128)}), f32[128,1,256]{2,1,0:T(1,128)S(1)}, u32[]{:S(2)}, u32[]{:S(2)}) %all-to-all-start.5) | async-done | bytes 131104 | tf_op jit(solution)/shard_map/all_to_all | solution.py:162
  428.1 52.7 %scatter_custom_fusion.3 = f32[32,32768]{0,1:T(8,128)} fusion(s32[8192]{0:T(1024)S(1)} %reshape.436, f32[]{:T(128)} %constant.111.clone.1, f32[32,1024]{0,1:T(8,128)S(1)} %bitcast_bitcast_fusion.1, f32[1024,8]{1,0:T(8,128)S(1)} %bitcast.269), kind=kCustom, calls=%fused_computation.102 | custom fusion | flops 524288 | bytes 5242884 | tf_op jit(solution)/shard_map/scatter-add | solution.py:166
  480.8 11.6 %copy.78 = f32[32,32768]{1,0:T(8,128)} copy(f32[32,32768]{0,1:T(8,128)} %scatter_custom_fusion.3) | data formatting | bytes 8388608 | tf_op jit(solution)/shard_map/scatter-add | solution.py:166
  492.4 5.8 %reshape.397 = f32[2,8,2,32768]{3,2,1,0:T(2,128)} reshape(f32[32,32768]{1,0:T(8,128)} %copy.78) | data formatting | bytes 8388608 | tf_op jit(solution)/shard_map/reshape | solution.py:168
  (481 shorter events, 237.8 us)
Async XLA Ops:
  9.9 53.5 %copy-start.10 = (s32[512,1]{0,1:T(1,128)}, s32[512,1]{0,1:T(1,128)S(1)}, u32[]{:S(2)}) copy-start(s32[512,1]{0,1:T(1,128)S(1)} %compare_select_fusion.5) | copy-start | bytes 6148
  13.2 52.6 %all-to-all-start = ((s32[128,8,1]{1,2,0:T(1,128)}), s32[128,8,1]{1,2,0:T(1,128)S(1)}, u32[]{:S(2)}, u32[]{:S(2)}) async-start(s32[128,8,1]{1,2,0:T(1,128)} %bitcast.10), calls=%async_computation | async-start | bytes 131072 | tf_op jit(solution)/shard_map/all_to_all | solution.py:134
  51.2 10.4 %copy-start.9 = (f32[8,512]{1,0:T(8,128)S(1)}, f32[8,512]{1,0:T(8,128)}, u32[]{:S(2)}) copy-start(f32[8,512]{1,0:T(8,128)} %param.21) | copy-start | bytes 49156
  65.8 44.1 %all-to-all-start.1 = ((f32[128,8,8]{2,1,0:T(8,128)}), f32[128,8,8]{2,1,0:T(8,128)S(1)}, u32[]{:S(2)}, u32[]{:S(2)}) async-start(f32[128,8,8]{2,1,0:T(8,128)} %bitcast.13), calls=%async_computation.1 | async-start | bytes 1048576 | tf_op jit(solution)/shard_map/all_to_all | solution.py:135
  110.0 28.2 %copy-start.5 = (f32[128,8,8]{2,1,0:T(8,128)}, f32[128,8,8]{2,1,0:T(8,128)S(1)}, u32[]{:S(2)}) copy-start(f32[128,8,8]{2,1,0:T(8,128)S(1)} %all-to-all-done.1) | copy-start | bytes 98308
  110.0 15.2 %all-to-all-start.3 = ((f32[16,1,1920]{2,1,0:T(1,128)}), f32[16,1,1920]{2,1,0:T(1,128)S(1)}, u32[]{:S(2)}, u32[]{:S(2)}) async-start(f32[16,1,1920]{2,1,0:T(1,128)} %reshape.523), calls=%async_computation.3 | async-start | bytes 245760 | tf_op jit(solution)/shard_map/all_to_all | solution.py:153
  125.2 20.1 %all-to-all-start.2 = ((f32[128,1,256]{2,1,0:T(1,128)}), f32[128,1,256]{2,1,0:T(1,128)S(1)}, u32[]{:S(2)}, u32[]{:S(2)}) async-start(f32[128,1,256]{2,1,0:T(1,128)} %reshape.527), calls=%async_computation.2 | async-start | bytes 262144 | tf_op jit(solution)/shard_map/all_to_all | solution.py:140
  145.3 261.9 %all-to-all-start.4 = ((f32[16,1,1920]{2,1,0:T(1,128)}), f32[16,1,1920]{2,1,0:T(1,128)}, u32[]{:S(2)}, u32[]{:S(2)}) async-start(f32[16,1,1920]{2,1,0:T(1,128)} %reshape.525), calls=%async_computation.4 | async-start | bytes 245760 | tf_op jit(solution)/shard_map/all_to_all | solution.py:155
  149.5 348.7 %all-reduce.4.cloned.1.call-start = ((), (), s32[]{:S(2)}) async-start(), calls=%async_computation.6 | async-start | bytes 2097152 | tf_op jit(solution)/shard_map/psum | solution.py:148
  245.7 4.7 copy-start.1
  245.7 4.7 copy-start.4
  251.3 6.6 %copy-start.8 = (f32[2,8,2,512]{3,2,0,1:T(2,128)S(1)}, f32[2,8,2,512]{3,2,0,1:T(2,128)}, u32[]{:S(2)}) copy-start(f32[2,8,2,512]{3,2,0,1:T(2,128)} %copy-done.7) | copy-start | bytes 196612 | tf_op jit(solution)/shard_map/while
  266.5 4.7 copy-start.1
  266.5 4.7 copy-start.4
  272.1 6.6 %copy-start.8 = (f32[2,8,2,512]{3,2,0,1:T(2,128)S(1)}, f32[2,8,2,512]{3,2,0,1:T(2,128)}, u32[]{:S(2)}) copy-start(f32[2,8,2,512]{3,2,0,1:T(2,128)} %copy-done.7) | copy-start | bytes 196612 | tf_op jit(solution)/shard_map/while
  287.3 4.6 copy-start.1
  292.8 6.6 %copy-start.8 = (f32[2,8,2,512]{3,2,0,1:T(2,128)S(1)}, f32[2,8,2,512]{3,2,0,1:T(2,128)}, u32[]{:S(2)}) copy-start(f32[2,8,2,512]{3,2,0,1:T(2,128)} %copy-done.7) | copy-start | bytes 196612 | tf_op jit(solution)/shard_map/while
  313.6 6.6 %copy-start.8 = (f32[2,8,2,512]{3,2,0,1:T(2,128)S(1)}, f32[2,8,2,512]{3,2,0,1:T(2,128)}, u32[]{:S(2)}) copy-start(f32[2,8,2,512]{3,2,0,1:T(2,128)} %copy-done.7) | copy-start | bytes 196612 | tf_op jit(solution)/shard_map/while
  328.8 4.6 copy-start.1
  328.8 4.6 copy-start.4
  334.4 6.6 %copy-start.8 = (f32[2,8,2,512]{3,2,0,1:T(2,128)S(1)}, f32[2,8,2,512]{3,2,0,1:T(2,128)}, u32[]{:S(2)}) copy-start(f32[2,8,2,512]{3,2,0,1:T(2,128)} %copy-done.7) | copy-start | bytes 196612 | tf_op jit(solution)/shard_map/while
  349.6 4.6 copy-start.1
  349.6 4.6 copy-start.4
  355.1 6.6 %copy-start.8 = (f32[2,8,2,512]{3,2,0,1:T(2,128)S(1)}, f32[2,8,2,512]{3,2,0,1:T(2,128)}, u32[]{:S(2)}) copy-start(f32[2,8,2,512]{3,2,0,1:T(2,128)} %copy-done.7) | copy-start | bytes 196612 | tf_op jit(solution)/shard_map/while
  370.3 4.7 copy-start.1
  370.3 4.7 copy-start.4
  375.9 6.6 %copy-start.8 = (f32[2,8,2,512]{3,2,0,1:T(2,128)S(1)}, f32[2,8,2,512]{3,2,0,1:T(2,128)}, u32[]{:S(2)}) copy-start(f32[2,8,2,512]{3,2,0,1:T(2,128)} %copy-done.7) | copy-start | bytes 196612 | tf_op jit(solution)/shard_map/while
  391.1 4.6 copy-start.1
  391.1 4.6 copy-start.4
  396.7 6.6 %copy-start.8 = (f32[2,8,2,512]{3,2,0,1:T(2,128)S(1)}, f32[2,8,2,512]{3,2,0,1:T(2,128)}, u32[]{:S(2)}) copy-start(f32[2,8,2,512]{3,2,0,1:T(2,128)} %copy-done.7) | copy-start | bytes 196612 | tf_op jit(solution)/shard_map/while
  407.2 19.7 %all-to-all-start.5 = ((f32[128,1,256]{2,1,0:T(1,128)}), f32[128,1,256]{2,1,0:T(1,128)S(1)}, u32[]{:S(2)}, u32[]{:S(2)}) async-start(f32[128,1,256]{2,1,0:T(1,128)} %reshape.529), calls=%async_computation.5 | async-start | bytes 262144 | tf_op jit(solution)/shard_map/all_to_all | solution.py:162
  419.0 9.1 %copy-start.6 = (f32[128,8,8]{2,1,0:T(8,128)S(1)}, f32[128,8,8]{2,1,0:T(8,128)}, u32[]{:S(2)}) copy-start(f32[128,8,8]{2,1,0:T(8,128)} %copy-done.5) | copy-start | bytes 98308
  (35 other events, 99.3 us)
Sparse Core Ops, SparseCore 0:
  407.3 62.3 all-reduce.3
where the time goes:
time: 516 us; the launch traced here: 507 us
  local copies, waits for them, and re-layouts  250 us (48%)
  other arithmetic  114 us (22%)
  starting transfers between devices  51.7 us (10%)
  matrix products  48.1 us (9%)
  blocking collectives  16 us (3%)
  between operations  14.6 us (3%)
  waiting for transfers between devices  8.97 us (2%)
    scatter-add x1, other arithmetic, body(): local_grid = jnp.zeros((grid_planes, grid_cells), jnp.float32).at[:, cell...  52.7 us
    gather x32, local copies, waits for them, and re-layouts, facet_parts(): right_gain = jnp.take(gain_slab, second_station, axis=0)  49.2 us
    gather x32, local copies, waits for them, and re-layouts, facet_parts(): left_gain = jnp.take(gain_slab, first_station, axis=0)  49.2 us
    gather x1, local copies, waits for them, and re-layouts, body(): tile_values = jnp.sum(grid_flat[:, cell_index] * got_taps[None], axis=2)  33.7 us
    dynamic_update_slice x8, local copies, waits for them, and re-layouts, add_grads(): lax.dynamic_update_index_in_dim(gain_acc, per_station.reshape(stations, 2...  32.3 us
    dot_general x16, matrix products, facet_parts(): jnp.einsum('xtr,tc->xrc', degrid_slab, spectrum, precision=lax.Precision....  21.4 us
    sub x24, other arithmetic, complex_mul(): return (x_re * y_re - x_im * y_im, x_re * y_im + x_im * y_re)  18.9 us
    reshape x2, local copies, waits for them, and re-layouts, body(): grid_flat = sky_grid.reshape(grid_planes, grid_cells)  16.4 us
  transfers between devices with their start and end apart: 7, of which 2 were waited for; matrix products, arithmetic and copies ran while one was open for 78% of the time, Pallas kernels for 0%

commit v1 on v0

v1 whole, which is shorter than its diff:
```python
import functools

import jax
import jax.numpy as jnp
from jax import lax
from jax.experimental import pallas as pl
from jax.experimental.pallas import tpu as pltpu
from jax.sharding import PartitionSpec as P

smoothness = 4.0
F32, BF16, I32 = jnp.float32, jnp.bfloat16, jnp.int32
LANES = 128
WORDS = 16
BLOCK = 512
STRIDE = LANES + 8
CHUNK = 16
VMEM_LIMIT = 56 << 20
NT = (((1,), (1,)), ((), ()))


def iota(shape, axis):
    return lax.broadcasted_iota(I32, shape, axis)


def halves(x):
    hi = x.astype(BF16)
    return hi, (x - hi.astype(F32)).astype(BF16)


def dot(x, y):
    return jnp.dot(x, y, preferred_element_type=F32)


def dot_nt(x, y):
    return lax.dot_general(x, y, NT, preferred_element_type=F32)


def ones_where(mask):
    return jnp.where(mask, 1.0, 0.0).astype(BF16)


def form_slots(owner_ref, offset_ref, taps_ref, place_ref, store_message):
    devices, rows = place_ref.shape[1:]
    hits = iota((devices, rows), 0) == owner_ref[...]
    earlier = ones_where(iota((rows, rows), 0) < iota((rows, rows), 1))
    counts = dot(ones_where(hits), earlier)
    rank = jnp.sum(jnp.where(hits, counts, 0.0), axis=0, keepdims=True)
    words = jnp.concatenate(
        [taps_ref[...], jnp.broadcast_to(offset_ref[...].astype(F32), (WORDS - 8, rows))], axis=0
    )
    hi, lo = halves(jnp.concatenate([words] * 8, axis=0))
    group = iota((devices, LANES), 1) // WORDS
    message = jnp.zeros((devices, LANES), F32)
    for j in range(8):
        place = ones_where(jnp.where(hits, rank, -1.0) == float(j))
        place_ref[j] = place
        message = jnp.where(group == j, dot_nt(place, hi) + dot_nt(place, lo), message)
    store_message(message)


def transpose_grid(stage_ref, cells_ref):
    blocks = stage_ref.shape[1] // 8

    @pl.loop(0, blocks)
    def _(b):
        tile = stage_ref[:, pl.ds(pl.multiple_of(b * 8, 8), 8), :].reshape(LANES, LANES)
        cells_ref[pl.ds(pl.multiple_of(b * STRIDE, 8), LANES), :] = tile.T

    quarter = (iota((8, LANES), 1) >> 1) & 3

    @pl.loop(0, blocks)
    def _(b):
        here = cells_ref[pl.ds(pl.multiple_of(b * STRIDE, 8), 8), :]
        after = cells_ref[pl.ds(pl.multiple_of(jnp.minimum(b + 1, blocks - 1) * STRIDE, 8), 8), :]
        pad = jnp.where(
            quarter < 3, pltpu.roll(here, LANES - 2, 1), pltpu.roll(after, 6, 1)
        )
        cells_ref[pl.ds(pl.multiple_of(b * STRIDE + LANES, 8), 8), :] = pad


def fold_table():
    a, b = iota((2 * LANES, LANES), 0) & (LANES - 1), iota((2 * LANES, LANES), 1)
    return ones_where(((a >> 3) == (b >> 3)) & ((a & 1) == (b & 1)))


def degrid_slots(offset_ref, words_ref, cells_ref, weight_ref, product_ref, store_value):
    sources = words_ref.shape[1]
    step = 4
    quarter = (iota((8, LANES), 1) >> 1) & 3

    @pl.loop(0, sources // step)
    def _(s0):
        first = s0 * step
        for j in range(8):
            taps = pltpu.roll(words_ref[j * WORDS : j * WORDS + 8, :], sources - first, 1)
            for i in range(step):
                offset = offset_ref[j, first + i]
                row = (offset >> 9) * STRIDE + (offset & (LANES - 1))
                lane = (offset >> 7) & 3
                weight = jnp.where(
                    quarter == lane, jnp.broadcast_to(taps[:, i : i + 1], (8, LANES)), 0.0
                )
                at = pl.ds(pl.multiple_of((first + i) * 64 + j * 8, 8), 8)
                weight_ref[at, :] = weight
                product_ref[at, :] = weight * cells_ref[pl.ds(row, 8), :]

    fold = fold_table()
    group = (iota((sources, LANES), 1) >> 1) & 3
    for h in range(2):
        value = jnp.zeros((sources, LANES), F32)
        for g in range(4):
            j = 4 * h + g
            total = product_ref[pl.ds(j * 8, sources, stride=64), :]
            for k in range(1, 8):
                total = total + product_ref[pl.ds(j * 8 + k, sources, stride=64), :]
            value = jnp.where(group == g, dot(jnp.concatenate(halves(total), axis=1), fold), value)
        store_value(h, value)


def gather_degrid(load_value, place_ref, part_ref, degrid_ref):
    sources = place_ref.shape[1]
    quarter = (iota((LANES, sources), 0) >> 1) & 3
    total = None
    for h in range(2):
        turned = load_value(h).T
        for pair in range(2):
            parts = [halves(jnp.where(quarter == g, turned, 0.0)) for g in (2 * pair, 2 * pair + 1)]
            j = 4 * h + 2 * pair
            place = place_ref[j : j + 2].reshape(2 * sources, place_ref.shape[2])
            for n in range(2):
                term = dot(jnp.concatenate([parts[0][n], parts[1][n]], axis=1), place)
                total = term if total is None else total + term
    for n in range(part_ref.shape[0]):
        tile = slice(n * LANES, (n + 1) * LANES)
        part_ref[n] = total[:, tile]
        for t in range(2):
            degrid_ref[t, :, tile] = sum(part_ref[n, pl.ds(2 * g + t, 16, stride=8), :] for g in range(4))


def station_tables(pairs_ref, gather_ref, sum_ref):
    rows = pairs_ref.shape[1]
    for side in range(2):
        hits = ((iota((LANES, rows), 0) & 63) == pairs_ref[side : side + 1, :]) * 1.0
        gather_ref[side] = hits.astype(BF16)
        turned = jnp.where(iota((rows, LANES), 1) < 64, hits.T, 0.0).astype(BF16)
        sum_ref[pl.ds(2 * side * rows, rows), :] = turned
        sum_ref[pl.ds((2 * side + 1) * rows, rows), :] = turned


def turn_gains(gains_ref, turned_ref):
    chunks = turned_ref.shape[0]
    for fc in range(16):
        tiles = []
        for lt in range(2):
            block = gains_ref[:, 2 * fc + lt, :]
            hi = block.astype(BF16).astype(F32)
            tiles.append(jnp.concatenate([hi, block - hi], axis=0).T)
        full = jnp.concatenate(tiles, axis=0)[: chunks * CHUNK].astype(BF16)
        turned_ref[:, fc // 2, fc % 2] = full.reshape(chunks, CHUNK, LANES)


def row_step(
    chunk, channels, vis_ref, scale_ref, degrid_ref, turned_ref, gather_ref, sum_ref,
    left_ref, right_ref, grads_ref, grad_degrid_ref, station_ref,
):
    facets = turned_ref.shape[1]
    rows = vis_ref.shape[2]
    gains = turned_ref[chunk].reshape(facets * 2 * CHUNK, LANES)
    left_ref[...] = dot(gains, gather_ref[0])
    right_ref[...] = dot(gains, gather_ref[1])
    channel = (iota((CHUNK, rows), 0) + chunk * CHUNK).astype(F32)
    ramp = 2.0 * channel / (channels - 1) - 1.0

    def parts(f):
        base = f * 2 * CHUNK
        re, im = slice(base, base + CHUNK), slice(base + CHUNK, base + 2 * CHUNK)
        model_re = degrid_ref[0, f : f + 1, :] + degrid_ref[1, f : f + 1, :] * ramp
        model_im = degrid_ref[0, facets + f : facets + f + 1, :] + degrid_ref[1, facets + f : facets + f + 1, :] * ramp
        return left_ref[re, :], left_ref[im, :], right_ref[re, :], right_ref[im, :], model_re, model_im

    pred_re = pred_im = None
    for f in range(facets):
        are, aim, bre, bim, mre, mim = parts(f)
        pre, pim = are * bre + aim * bim, aim * bre - are * bim
        vre, vim = pre * mre - pim * mim, pre * mim + pim * mre
        pred_re = vre if pred_re is None else pred_re + vre
        pred_im = vim if pred_im is None else pred_im + vim
    at = pl.ds(pl.multiple_of(chunk * CHUNK, CHUNK), CHUNK)
    ere = scale_ref[...] * (pred_re - vis_ref[0, at, :].astype(F32))
    eim = scale_ref[...] * (pred_im - vis_ref[1, at, :].astype(F32))
    for f in range(facets):
        are, aim, bre, bim, mre, mim = parts(f)
        base = f * 2 * CHUNK
        qre, qim = ere * mre + eim * mim, eim * mre - ere * mim
        values = (
            (qre * bre - qim * bim, qre * bim + qim * bre),
            (qre * are + qim * aim, qre * aim - qim * are),
        )
        for side in range(2):
            for c in range(2):
                hi, lo = halves(values[side][c])
                to = slice(base + c * CHUNK, base + (c + 1) * CHUNK)
                grads_ref[to, pl.ds(2 * side * rows, rows)] = hi
                grads_ref[to, pl.ds((2 * side + 1) * rows, rows)] = lo
        pre, pim = are * bre + aim * bim, aim * bre - are * bim
        models = (ere * pre + eim * pim, eim * pre - ere * pim)
        for c in range(2):
            n = c * facets + f
            slope = models[c] * ramp
            grad_degrid_ref[0, n] += models[c][:8] + models[c][8:]
            grad_degrid_ref[1, n] += slope[:8] + slope[8:]
    station_ref[chunk] = dot(grads_ref[...], sum_ref[...])


def place_grads(grad_degrid_ref, place_ref, store_value):
    planes = grad_degrid_ref.shape[1]
    rows = grad_degrid_ref.shape[3]
    devices = place_ref.shape[1]
    odd = (iota((8, rows), 0) & 1) == 1
    full = []
    for n in range(planes):
        level = jnp.sum(grad_degrid_ref[0, n], axis=0, keepdims=True)
        slope = jnp.sum(grad_degrid_ref[1, n], axis=0, keepdims=True)
        full.append(jnp.where(odd, slope, level))
    hi, lo = halves(jnp.concatenate(full, axis=0))
    group = (iota((devices, LANES), 1) >> 1) & 3
    for h in range(2):
        value = jnp.zeros((devices, LANES), F32)
        for g in range(4):
            place = place_ref[4 * h + g]
            value = jnp.where(group == g, dot_nt(place, hi) + dot_nt(place, lo), value)
        store_value(h, value)


def split_stations(station_ref, out_ref):
    chunks = station_ref.shape[0]
    for fc in range(16):
        block = station_ref[:, fc * CHUNK : (fc + 1) * CHUNK, :].reshape(chunks * CHUNK, LANES)
        block = jnp.concatenate([block, jnp.zeros((2 * LANES - chunks * CHUNK, LANES), F32)], axis=0)
        for lt in range(2):
            turned = block[lt * LANES : (lt + 1) * LANES].T
            out_ref[:, fc, :, pl.ds(lt * LANES, LANES)] = turned[:64].reshape(8, 8, LANES)


def form_kernel(owner_ref, offset_ref, taps_ref, place_ref, message_ref):
    def store(message):
        message_ref[...] = message

    form_slots(owner_ref, offset_ref, taps_ref, place_ref, store)


def degrid_kernel(offset_ref, message_ref, sky_ref, weight_ref, value_ref, stage, words, cells, product, sem):
    copy = pltpu.make_async_copy(sky_ref, stage, sem)
    copy.start()
    words[...] = message_ref[...].T
    copy.wait()
    transpose_grid(stage, cells)

    def store(h, value):
        value_ref[:, h, :] = value

    degrid_slots(offset_ref, words, cells, weight_ref, product, store)


def rows_kernel(
    value_ref, place_ref, gains_ref, vis_ref, noise_ref, keep_ref, pairs_ref,
    grad_ref, out_ref,
    part, degrid, turned, gather, sums, scale, left, right, grads, grad_degrid, station,
    channels,
):
    scale[...] = noise_ref[...] * keep_ref[...].astype(F32)
    station_tables(pairs_ref, gather, sums)
    turn_gains(gains_ref, turned)
    gather_degrid(lambda h: value_ref[:, h, :], place_ref, part, degrid)
    grad_degrid[...] = jnp.zeros_like(grad_degrid)

    @pl.loop(0, turned.shape[0])
    def _(chunk):
        row_step(
            chunk, channels, vis_ref, scale, degrid, turned, gather, sums,
            left, right, grads, grad_degrid, station,
        )

    def store(h, value):
        grad_ref[:, h, :] = value

    place_grads(grad_degrid, place_ref, store)
    split_stations(station, out_ref)


def scatter_kernel(offset_ref, weight_ref, grad_ref, sky_ref, spread, cells, stage, sem):
    sources = grad_ref.shape[0]
    blocks = stage.shape[1] // 8
    fold = fold_table()
    group = (iota((sources, LANES), 1) >> 1) & 3
    for h in range(2):
        block = grad_ref[:, h, :]
        for g in range(4):
            part = jnp.concatenate(halves(jnp.where(group == g, block, 0.0)), axis=1)
            spread[pl.ds(4 * h + g, sources, stride=8), :] = dot(part, fold)

    @pl.loop(0, blocks)
    def _(b):
        at = pl.ds(pl.multiple_of(b * STRIDE, 8), STRIDE)
        for n in range(2):
            cells[n, at, :] = jnp.zeros((STRIDE, LANES), F32)

    @pl.loop(0, sources)
    def _(s):
        for j in range(8):
            offset = offset_ref[j, s]
            row = (offset >> 9) * STRIDE + (offset & (LANES - 1))
            at = pl.ds(pl.multiple_of(s * 64 + j * 8, 8), 8)
            term = weight_ref[at, :] * spread[pl.ds(s * 8 + j, 1), :]
            cells[j % 2, pl.ds(row, 8), :] += term

    quarter = (iota((8, LANES), 1) >> 1) & 3

    @pl.loop(0, blocks)
    def _(b):
        at = pl.ds(pl.multiple_of(b * STRIDE, 8), LANES)
        tile = cells[0, at, :] + cells[1, at, :]
        pads = pl.ds(pl.multiple_of(b * STRIDE + LANES, 8), 8)
        before = pl.ds(pl.multiple_of(jnp.maximum(b - 1, 0) * STRIDE + LANES, 8), 8)
        here = pltpu.roll(cells[0, pads, :] + cells[1, pads, :], 2, 1)
        last = pltpu.roll(cells[0, before, :] + cells[1, before, :], LANES - 6, 1)
        last = jnp.where(b > 0, last, 0.0)
        head = tile[:8] + jnp.where(quarter > 0, here, last)
        turned = jnp.concatenate([head, tile[8:]], axis=0).T
        stage[:, pl.ds(pl.multiple_of(b * 8, 8), 8), :] = turned.reshape(16, 8, LANES)

    copy = pltpu.make_async_copy(stage, sky_ref, sem)
    copy.start()
    copy.wait()


def vmem(count):
    return [pl.BlockSpec(memory_space=pltpu.VMEM)] * count


def shape(dims, dtype=F32):
    return jax.ShapeDtypeStruct(dims, dtype)


def params():
    return pltpu.CompilerParams(vmem_limit_bytes=VMEM_LIMIT)


def body(
    visibilities, noise_weight, keep_flag, station_pairs, tile_owner, tile_offset, kernel_taps, gain_field, sky_grid
):
    rows = visibilities.shape[0]
    channels = visibilities.shape[2]
    devices = lax.axis_size("tm") * lax.axis_size("bl")
    chunks = channels // CHUNK
    parts, facets, terms, cells = sky_grid.shape
    lines = cells // LANES
    sky = sky_grid.reshape(parts, facets, terms, lines, LANES).transpose(0, 1, 3, 2, 4)
    sky = sky.reshape(parts * facets, lines * terms, LANES)

    place, message = pl.pallas_call(
        form_kernel,
        out_shape=(shape((8, devices, rows), BF16), shape((devices, LANES))),
        in_specs=vmem(3),
        out_specs=tuple(vmem(2)),
        compiler_params=params(),
        name="form",
    )(tile_owner.reshape(1, rows), tile_offset.reshape(1, rows), kernel_taps)
    got = lax.all_to_all(message, ("tm", "bl"), split_axis=0, concat_axis=0, tiled=True)
    offsets = got.reshape(devices, 8, WORDS)[:, :, 8].T.astype(I32)

    weight, value = pl.pallas_call(
        degrid_kernel,
        out_shape=(shape((devices * 64, LANES)), shape((devices, 2, LANES))),
        in_specs=[pl.BlockSpec(memory_space=pltpu.SMEM)] + vmem(1) + [pl.BlockSpec(memory_space=pl.ANY)],
        out_specs=tuple(vmem(2)),
        scratch_shapes=[
            pltpu.VMEM(sky.shape, F32),
            pltpu.VMEM((LANES, devices), F32),
            pltpu.VMEM((cells // BLOCK * STRIDE, LANES), F32),
            pltpu.VMEM((devices * 64, LANES), F32),
            pltpu.SemaphoreType.DMA,
        ],
        compiler_params=params(),
        name="degrid",
    )(offsets, got, sky)
    value = lax.all_to_all(value, ("tm", "bl"), split_axis=0, concat_axis=0, tiled=True)

    own = jnp.pad(gain_field[0], ((0, 0), (0, 0), (0, 0), (0, 2 * LANES - channels)))
    own = own.reshape(-1, facets * 4, LANES)
    gains = lax.all_gather(own, "bl", axis=0, tiled=True)
    grad, partial = pl.pallas_call(
        functools.partial(rows_kernel, channels=channels),
        out_shape=(shape((devices, 2, LANES)), shape((8, 16, 8, 2 * LANES))),
        in_specs=vmem(7),
        out_specs=tuple(vmem(2)),
        scratch_shapes=[
            pltpu.VMEM((rows // LANES, LANES, LANES), F32),
            pltpu.VMEM((2, 16, rows), F32),
            pltpu.VMEM((chunks, facets, 2, CHUNK, LANES), BF16),
            pltpu.VMEM((2, LANES, rows), BF16),
            pltpu.VMEM((4 * rows, LANES), BF16),
            pltpu.VMEM((1, rows), F32),
            pltpu.VMEM((facets * 2 * CHUNK, rows), F32),
            pltpu.VMEM((facets * 2 * CHUNK, rows), F32),
            pltpu.VMEM((facets * 2 * CHUNK, 4 * rows), BF16),
            pltpu.VMEM((2, 2 * facets, 8, rows), F32),
            pltpu.VMEM((chunks, facets * 2 * CHUNK, LANES), F32),
        ],
        compiler_params=params(),
        name="rows",
    )(
        value, place, gains, visibilities.transpose(1, 2, 0), noise_weight.reshape(1, rows),
        keep_flag.reshape(1, rows), station_pairs,
    )
    grad = lax.all_to_all(grad, ("tm", "bl"), split_axis=0, concat_axis=0, tiled=True)
    data = lax.psum_scatter(partial, "bl", scatter_dimension=0, tiled=False)

    out_grid = pl.pallas_call(
        scatter_kernel,
        out_shape=shape(sky.shape),
        in_specs=[pl.BlockSpec(memory_space=pltpu.SMEM)] + vmem(2),
        out_specs=pl.BlockSpec(memory_space=pl.ANY),
        scratch_shapes=[
            pltpu.VMEM((devices * 8, LANES), F32),
            pltpu.VMEM((2, cells // BLOCK * STRIDE, LANES), F32),
            pltpu.VMEM(sky.shape, F32),
            pltpu.SemaphoreType.DMA,
        ],
        compiler_params=params(),
        name="scatter",
    )(offsets, weight, grad)
    grid_gradient = out_grid.reshape(parts, facets, lines, terms, LANES).transpose(0, 1, 3, 2, 4)
    grid_gradient = grid_gradient.reshape(sky_grid.shape)

    times = lax.axis_size("tm")
    below = lax.ppermute(gain_field, "tm", [(i, i + 1) for i in range(times - 1)])
    above = lax.ppermute(gain_field, "tm", [(i + 1, i) for i in range(times - 1)])
    here = lax.axis_index("tm")
    smooth = jnp.where(here > 0, gain_field - below, 0.0) - jnp.where(here < times - 1, above - gain_field, 0.0)
    data = data.reshape(facets, 2, 8, 2 * LANES).transpose(2, 0, 1, 3)[None, :, :, :, :channels]
    return (data + smoothness * smooth, grid_gradient)


def solution(mesh):
    split = ("tm", "bl")
    return jax.shard_map(
        body,
        mesh=mesh,
        in_specs=(
            P(split, None, None),
            P(split),
            P(split),
            P(None, split),
            P(split, None),
            P(split),
            P(None, split),
            P("tm", "bl", None, None, None),
            P(None, None, None, split),
        ),
        out_specs=(P("tm", "bl", None, None, None), P(None, None, None, split)),
        check_vma=False,
    )
```

time: 516 us -> 138 us (0.27); the launches traced: 507 us -> 138 us
  local copies, waits for them, and re-layouts: 250 us -> 3.44 us
  other arithmetic: 114 us -> 1.43 us
  Pallas kernels: 0 us -> 68 us
  matrix products: 48.1 us -> 0 us
  starting transfers between devices: 51.7 us -> 9.19 us
  blocking collectives: 16 us -> 36.6 us
    gather x67 -> x0, local copies, waits for them, and re-layouts: 133 us -> none  [the longest x32 49.2 us: facet_parts(): right_gain = jnp.take(gain_slab, second_station, axis=0)]
    pallas_call x0 -> x4, Pallas kernels: none -> 68 us  [the longest x1 23.2 us: body(): pl.pallas_call(degrid_kernel, out_shape=(shape((devices * 64, LANES)), sh...]
    scatter-add x1 -> x0, other arithmetic: 52.7 us -> none  [body(): local_grid = jnp.zeros((grid_planes, grid_cells), jnp.float32).at[:, cell...]
    dot_general x40 -> x0, matrix products: 48.1 us -> none  [the longest x16 21.4 us: facet_parts(): jnp.einsum('xtr,tc->xrc', degrid_slab, spectrum, precision=lax.Precision....]
    all_to_all x6 -> x1, starting transfers between devices: 51.6 us -> 4.52 us  [body(): lax.all_to_all(grad, ('tm', 'bl'), split_axis=0, concat_axis=0, tiled=True)]
    all_to_all x0 -> x2, blocking collectives: none -> 36.6 us  [the longest x1 20.8 us: body(): lax.all_to_all(message, ('tm', 'bl'), split_axis=0, concat_axis=0, tiled=...]
    dynamic_update_slice x8 -> x0, local copies, waits for them, and re-layouts: 32.3 us -> none  [add_grads(): lax.dynamic_update_index_in_dim(gain_acc, per_station.reshape(stations, 2...]
    reshape x6 -> x1, local copies, waits for them, and re-layouts: 23.3 us -> 0.76 us  [body(): own = own.reshape(-1, facets * 4, LANES)]
  transfers between devices with their start and end apart: 7 -> 5, of which waited for: 2 -> 1; matrix products, arithmetic and copies ran while one was open for 78% -> 1% of each run, Pallas kernels for 0% -> 33%
where the time goes in v1:
time: 138 us
  Pallas kernels  68 us (49%)
  blocking collectives  36.6 us (27%)
  between operations  14.1 us (10%)
  starting transfers between devices  9.19 us (7%)
  waiting for transfers between devices  5.19 us (4%)
  local copies, waits for them, and re-layouts  3.44 us (2%)
  other arithmetic  1.43 us (1%)
    pallas_call x1, Pallas kernels, body(): pl.pallas_call(degrid_kernel, out_shape=(shape((devices * 64, LANES)), sh...  23.2 us
    pallas_call x1, Pallas kernels, body(): pl.pallas_call(functools.partial(rows_kernel, channels=channels), out_sha...  22.2 us
    all_to_all x1, blocking collectives, body(): lax.all_to_all(message, ('tm', 'bl'), split_axis=0, concat_axis=0, tiled=...  20.8 us
    pallas_call x1, Pallas kernels, body(): pl.pallas_call(scatter_kernel, out_shape=shape(sky.shape), in_specs=[pl.B...  20.3 us
    all_to_all x1, blocking collectives, body(): lax.all_to_all(value, ('tm', 'bl'), split_axis=0, concat_axis=0, tiled=True)  15.8 us
    all_to_all x1, waiting for transfers between devices, body(): lax.all_to_all(grad, ('tm', 'bl'), split_axis=0, concat_axis=0, tiled=True)  5.13 us
    all_to_all x1, starting transfers between devices, body(): lax.all_to_all(grad, ('tm', 'bl'), split_axis=0, concat_axis=0, tiled=True)  4.52 us
    ppermute x1, starting transfers between devices, body(): lax.ppermute(gain_field, 'tm', [(i, i + 1) for i in range(times - 1)])  3.3 us
  transfers between devices with their start and end apart: 5, of which 1 were waited for; matrix products, arithmetic and copies ran while one was open for 1% of the time, Pallas kernels for 33%

profile of v1, /device:TPU:1, one launch (start us, length us, event | category | flops | bytes accessed | tf_op | source)
XLA Modules:
  0.0 138.0 jit_solution(10923520238850838021)
XLA Ops:
  7.2 0.0 all-gather.2.cloned.1.call-start
  7.2 1.0 pad.4
  8.2 0.8 reshape.43
  8.9 0.0 all-gather.2.cloned.1.call-update
  9.0 0.0 reduce-scatter.2.cloned.1.call-start
  9.0 2.4 %form.1 = (bf16[8,128,512]{2,1,0:T(8,128)(2,1)}, f32[128,128]{1,0:T(8,128)}) custom-call(s32[1,512]{1,0:T(1,128)} %bitcast.44, s32[1,512]{1,0:T(1,128)} %bitcast.45, f32[8,512]{1,0:T(8,128)} %taps_ref.1), custom_call_target="tpu_custom_call" | custom-call | tf_op jit(solution)/shard_map/form/pallas_call | solution.py:361
  11.4 20.8 %all_to_all.21 = f32[128,1,128]{2,1,0:T(1,128)S(1)} all-to-all(f32[128,1,128]{2,1,0:T(1,128)} %bitcast.42), channel_id=1, replica_groups=mesh['tm'=16,'bl'=8] {'tm','bl'}, dimensions={0} | all-to-all | bytes 131072 | tf_op jit(solution)/shard_map/all_to_all | solution.py:369
  32.2 0.0 copy-start
  32.2 0.1 copy.20
  32.3 0.6 convert_bitcast_fusion.offset_ref
  32.9 0.0 copy-done
  32.9 0.0 copy-start.2
  32.9 23.2 %degrid.1 = (f32[8192,128]{1,0:T(8,128)}, f32[128,2,128]{2,1,0:T(2,128)}) custom-call(s32[8,128]{1,0:T(8,128)} %convert_bitcast_fusion.offset_ref, f32[128,128]{1,0:T(8,128)} %bitcast.36, f32[16,512,128]{2,1,0:T(8,128)} %bitcast.34), custom_call_target="tpu_custom_call" | custom-call | tf_op jit(solution)/shard_map/degrid/pallas_call | solution.py:372
  56.1 15.8 %all_to_all.22.value_ref = f32[128,2,128]{2,1,0:T(2,128)} all-to-all(f32[128,2,128]{2,1,0:T(2,128)} %get-tuple-element.9), channel_id=1, replica_groups=mesh['tm'=16,'bl'=8] {'tm','bl'}, dimensions={0} | all-to-all | bytes 262144 | tf_op jit(solution)/shard_map/all_to_all | solution.py:387
  71.9 0.0 all-gather.2.cloned.1.call-done.gains_ref
  71.9 22.2 %rows.1 = (f32[128,2,128]{2,1,0:T(2,128)}, f32[8,16,8,256]{3,2,1,0:T(8,128)}) custom-call(f32[128,2,128]{2,1,0:T(2,128)} %all_to_all.22.value_ref, bf16[8,128,512]{2,1,0:T(8,128)(2,1)} %get-tuple-element.10.place_ref, f32[64,32,128]{2,1,0:T(8,128)} %all-gather.2.cloned.1.call-done.gains_ref, bf16[2,240,512]{2,1,0:T(8,128)(2,1)} %bitcast.39, ...), custom_call_target="tpu_custom_call" | custom-call | tf_op jit(solution)/shard_map/rows/pallas_call | solution.py:392
  94.1 0.0 reduce-scatter.2.cloned.1.call-update
  94.1 4.5 %all-to-all-start.2 = ((f32[128,2,128]{2,1,0:T(2,128)}), f32[128,2,128]{2,1,0:T(2,128)S(1)}, u32[]{:S(2)}, u32[]{:S(2)}) async-start(f32[128,2,128]{2,1,0:T(2,128)} %get-tuple-element.13), calls=%async_computation.3 | async-start | bytes 262144 | tf_op jit(solution)/shard_map/all_to_all | solution.py:416
  98.6 0.0 copy-done.2
  98.6 3.3 %collective-permute-start = (f32[1,8,8,2,240]{4,3,2,1,0:T(2,128)S(1)}, f32[1,8,8,2,240]{4,3,2,1,0:T(2,128)S(1)}, u32[]{:S(2)}, u32[]{:S(2)}) collective-permute-start(f32[1,8,8,2,240]{4,3,2,1,0:T(2,128)S(1)} %copy-done.2), channel_id=1, source_target_pairs={{0,8},{8,16},{16,24},{24,32},{32,40},{40,48},{48,56},{56,64},{64,7... | collective-permute-start | bytes 368648 | tf_op jit(solution)/shard_map/ppermute | solution.py:437
  101.9 1.3 collective-permute-start.1
  103.2 5.1 %all-to-all-done.2.grad_ref = f32[128,2,128]{2,1,0:T(2,128)S(1)} async-done(((f32[128,2,128]{2,1,0:T(2,128)}), f32[128,2,128]{2,1,0:T(2,128)S(1)}, u32[]{:S(2)}, u32[]{:S(2)}) %all-to-all-start.2) | async-done | bytes 131104 | tf_op jit(solution)/shard_map/all_to_all | solution.py:416
  108.4 0.0 copy-start.1
  108.4 0.7 copy-done.1
  109.0 20.3 %scatter.1 = f32[16,512,128]{2,1,0:T(8,128)} custom-call(s32[8,128]{1,0:T(8,128)} %convert_bitcast_fusion.offset_ref, f32[8192,128]{1,0:T(8,128)} %get-tuple-element.12.weight_ref, f32[128,2,128]{2,1,0:T(2,128)} %copy-done.1), custom_call_target="tpu_custom_call" | custom-call | tf_op jit(solution)/shard_map/scatter/pallas_call | solution.py:419
  129.3 0.0 reduce-scatter.2.cloned.1.call-done
  129.3 1.0 copy.27
  130.3 0.0 collective-permute-done
  130.3 0.0 collective-permute-done.1
  130.3 0.8 fusion
  (1 shorter events, 0.0 us)
Async XLA Ops:
  7.2 64.7 %all-gather.2.cloned.1.call-start = ((), (), s32[]{:S(2)}) async-start(), calls=%async_computation.4 | async-start | bytes 1179648 | tf_op jit(solution)/shard_map/all_gather | solution.py:391
  9.0 120.4 %reduce-scatter.2.cloned.1.call-start = ((), (), s32[]{:S(2)}) async-start(), calls=%async_computation.5 | async-start | bytes 1179648 | tf_op jit(solution)/shard_map/reduce_scatter | solution.py:417
  32.2 0.7 copy-start
  32.9 65.7 %copy-start.2 = (f32[1,8,8,2,240]{4,3,2,1,0:T(2,128)S(1)}, f32[1,8,8,2,240]{4,3,2,1,0:T(2,128)}, u32[]{:S(2)}) copy-start(f32[1,8,8,2,240]{4,3,2,1,0:T(2,128)} %param.16) | copy-start | bytes 368644
  94.1 14.3 %all-to-all-start.2 = ((f32[128,2,128]{2,1,0:T(2,128)}), f32[128,2,128]{2,1,0:T(2,128)S(1)}, u32[]{:S(2)}, u32[]{:S(2)}) async-start(f32[128,2,128]{2,1,0:T(2,128)} %get-tuple-element.13), calls=%async_computation.3 | async-start | bytes 262144 | tf_op jit(solution)/shard_map/all_to_all | solution.py:416
  98.6 31.7 %collective-permute-start = (f32[1,8,8,2,240]{4,3,2,1,0:T(2,128)S(1)}, f32[1,8,8,2,240]{4,3,2,1,0:T(2,128)S(1)}, u32[]{:S(2)}, u32[]{:S(2)}) collective-permute-start(f32[1,8,8,2,240]{4,3,2,1,0:T(2,128)S(1)} %copy-done.2), channel_id=1, source_target_pairs={{0,8},{8,16},{16,24},{24,32},{32,40},{40,48},{48,56},{56,64},{64,7... | collective-permute-start | bytes 368648 | tf_op jit(solution)/shard_map/ppermute | solution.py:437
  101.9 28.4 %collective-permute-start.1 = (f32[1,8,8,2,240]{4,3,2,1,0:T(2,128)S(1)}, f32[1,8,8,2,240]{4,3,2,1,0:T(2,128)S(1)}, u32[]{:S(2)}, u32[]{:S(2)}) collective-permute-start(f32[1,8,8,2,240]{4,3,2,1,0:T(2,128)S(1)} %copy-done.2), channel_id=1, source_target_pairs={{8,0},{16,8},{24,16},{32,24},{40,32},{48,40},{56,48},{64,56},{72,6... | collective-permute-start | bytes 368648 | tf_op jit(solution)/shard_map/ppermute | solution.py:438
  108.4 0.7 copy-start.1
Sparse Core Ops, SparseCore 0:
  9.7 27.2 all-gather.1
  94.2 25.7 reduce-scatter.1

commit v2 on v1

v2 whole, which is shorter than its diff:
```python
import functools

import jax
import jax.numpy as jnp
from jax import lax
from jax.experimental import pallas as pl
from jax.experimental.pallas import tpu as pltpu
from jax.sharding import PartitionSpec as P

smoothness = 4.0
F32, BF16, I32 = jnp.float32, jnp.bfloat16, jnp.int32
LANES = 128
WORDS = 16
BLOCK = 512
STRIDE = LANES + 8
CHUNK = 16
VMEM_LIMIT = 56 << 20
NT = (((1,), (1,)), ((), ()))


def iota(shape, axis):
    return lax.broadcasted_iota(I32, shape, axis)


def halves(x):
    hi = x.astype(BF16)
    return hi, (x - hi.astype(F32)).astype(BF16)


def dot(x, y):
    return jnp.dot(x, y, preferred_element_type=F32)


def dot_nt(x, y):
    return lax.dot_general(x, y, NT, preferred_element_type=F32)


def ones_where(mask):
    return jnp.where(mask, 1.0, 0.0).astype(BF16)


def form_slots(owner_ref, offset_ref, taps_ref, place_ref, store_message):
    devices, rows = place_ref.shape[1:]
    hits = iota((devices, rows), 0) == owner_ref[...]
    earlier = ones_where(iota((rows, rows), 0) < iota((rows, rows), 1))
    counts = dot(ones_where(hits), earlier)
    rank = jnp.sum(jnp.where(hits, counts, 0.0), axis=0, keepdims=True)
    offset = offset_ref[...]
    row = (offset >> 9) * STRIDE + (offset & (LANES - 1))
    tail = jnp.where(iota((WORDS - 8, rows), 0) == 0, row, (offset >> 7) & 3).astype(F32)
    words = jnp.concatenate([taps_ref[...], tail], axis=0)
    hi, lo = halves(jnp.concatenate([words] * 8, axis=0))
    group = iota((devices, LANES), 1) // WORDS
    message = jnp.zeros((devices, LANES), F32)
    for j in range(8):
        place = ones_where(jnp.where(hits, rank, -1.0) == float(j))
        place_ref[j] = place
        message = jnp.where(group == j, dot_nt(place, hi) + dot_nt(place, lo), message)
    store_message(message)


def transpose_grid(stage_ref, cells_ref):
    blocks = stage_ref.shape[1] // 8

    @pl.loop(0, blocks, unroll=8)
    def _(b):
        tile = stage_ref[:, pl.ds(pl.multiple_of(b * 8, 8), 8), :].reshape(LANES, LANES)
        cells_ref[pl.ds(pl.multiple_of(b * STRIDE, 8), LANES), :] = tile.T

    quarter = (iota((8, LANES), 1) >> 1) & 3
    for b in range(blocks):
        here = cells_ref[b * STRIDE : b * STRIDE + 8, :]
        next_block = min(b + 1, blocks - 1) * STRIDE
        after = cells_ref[next_block : next_block + 8, :]
        pad = jnp.where(quarter < 3, pltpu.roll(here, LANES - 2, 1), pltpu.roll(after, 6, 1))
        cells_ref[b * STRIDE + LANES : (b + 1) * STRIDE, :] = pad


def spread_taps(words_ref, weight_ref):
    sources = words_ref.shape[0]
    tall = jnp.broadcast_to(words_ref[...].reshape(sources, 1, LANES), (sources, 8, LANES)).reshape(8 * sources, LANES)
    tall = jnp.where((iota(tall.shape, 1) & (WORDS - 1)) == (iota(tall.shape, 0) & 7), tall, 0.0)
    both = jnp.concatenate(halves(tall), axis=1)
    for pair in range(4):
        a, b = iota((2 * LANES, 2 * LANES), 0) & (LANES - 1), iota((2 * LANES, 2 * LANES), 1)
        weight = dot(both, ones_where(a // WORDS == 2 * pair + b // LANES))
        for n in range(2):
            weight_ref[2 * pair + n] = weight[:, n * LANES : (n + 1) * LANES]


def slot_quarter(words_ref, j):
    return jnp.broadcast_to(words_ref[:, j * WORDS + 9 : j * WORDS + 10], (words_ref.shape[0], LANES))


def fold_table():
    a, b = iota((2 * LANES, LANES), 0) & (LANES - 1), iota((2 * LANES, LANES), 1)
    return ones_where(((a >> 3) == (b >> 3)) & ((a & 1) == (b & 1)))


def degrid_slots(first_ref, words_ref, cells_ref, weight_ref, product_ref, store_value):
    sources = words_ref.shape[0]

    @pl.loop(0, sources, unroll=2)
    def _(s):
        at = pl.ds(pl.multiple_of(s * 8, 8), 8)
        for j in range(8):
            product_ref[j, at, :] = weight_ref[j, at, :] * cells_ref[pl.ds(first_ref[j, s], 8), :]

    fold = fold_table()
    lane_quarter = (iota((sources, LANES), 1) >> 1) & 3
    for h in range(2):
        value = jnp.zeros((sources, LANES), F32)
        for g in range(4):
            j = 4 * h + g
            total = product_ref[j, pl.ds(0, sources, stride=8), :]
            for k in range(1, 8):
                total = total + product_ref[j, pl.ds(k, sources, stride=8), :]
            total = jnp.where(slot_quarter(words_ref, j) == lane_quarter.astype(F32), total, 0.0)
            value = jnp.where(lane_quarter == g, dot(jnp.concatenate(halves(total), axis=1), fold), value)
        store_value(h, value)


def gather_degrid(load_value, place_ref, part_ref, degrid_ref):
    sources = place_ref.shape[1]
    quarter = (iota((LANES, sources), 0) >> 1) & 3
    total = None
    for h in range(2):
        turned = load_value(h).T
        for pair in range(2):
            parts = [halves(jnp.where(quarter == g, turned, 0.0)) for g in (2 * pair, 2 * pair + 1)]
            j = 4 * h + 2 * pair
            place = place_ref[j : j + 2].reshape(2 * sources, place_ref.shape[2])
            for n in range(2):
                term = dot(jnp.concatenate([parts[0][n], parts[1][n]], axis=1), place)
                total = term if total is None else total + term
    for n in range(part_ref.shape[0]):
        tile = slice(n * LANES, (n + 1) * LANES)
        part_ref[n] = total[:, tile]
        for t in range(2):
            degrid_ref[t, :, tile] = sum(part_ref[n, pl.ds(2 * g + t, 16, stride=8), :] for g in range(4))


def station_tables(pairs_ref, gather_ref, sum_ref):
    rows = pairs_ref.shape[1]
    for side in range(2):
        hits = ones_where((iota((LANES, rows), 0) & 63) == pairs_ref[side : side + 1, :])
        gather_ref[side] = hits
        for n in range(2):
            sum_ref[:, (2 * side + n) * rows : (2 * side + n + 1) * rows] = hits[:64]


def turn_gains(gains_ref, turned_ref, channels):
    for fc in range(16):
        tiles = []
        for lt in range(2):
            block = gains_ref[:, 2 * fc + lt, :]
            hi = block.astype(BF16).astype(F32)
            tiles.append(jnp.concatenate([hi, block - hi], axis=0).T)
        turned_ref[fc * channels : (fc + 1) * channels] = jnp.concatenate(tiles, axis=0)[:channels].astype(BF16)


def gather_gains(turned_ref, gather_ref, left_ref, right_ref):
    size = turned_ref.shape[0] // 3

    @pl.loop(0, 3)
    def _(n):
        at = pl.ds(pl.multiple_of(n * size, CHUNK), size)
        gains = turned_ref[at, :]
        left_ref[at, :] = dot(gains, gather_ref[0])
        right_ref[at, :] = dot(gains, gather_ref[1])


def row_step(chunk, channels, vis_ref, scale_ref, degrid_ref, left_ref, right_ref, grads_ref, grad_degrid_ref):
    rows = vis_ref.shape[2]
    facets = left_ref.shape[0] // channels // 2
    width = 2 * LANES

    def rows_of(n):
        return pl.ds(pl.multiple_of(n * channels + chunk * CHUNK, CHUNK), CHUNK)

    at = rows_of(0)
    channel = (iota((CHUNK, width), 0) + chunk * CHUNK).astype(F32)
    ramp = 2.0 * channel / (channels - 1) - 1.0
    for lanes in range(rows // width):
        ln = slice(lanes * width, (lanes + 1) * width)

        def parts(f):
            re, im = rows_of(2 * f), rows_of(2 * f + 1)
            g = facets + f
            mre = degrid_ref[0, f : f + 1, ln] + degrid_ref[1, f : f + 1, ln] * ramp
            mim = degrid_ref[0, g : g + 1, ln] + degrid_ref[1, g : g + 1, ln] * ramp
            return left_ref[re, ln], left_ref[im, ln], right_ref[re, ln], right_ref[im, ln], mre, mim

        pred_re = pred_im = None
        for f in range(facets):
            are, aim, bre, bim, mre, mim = parts(f)
            pre, pim = are * bre + aim * bim, aim * bre - are * bim
            vre, vim = pre * mre - pim * mim, pre * mim + pim * mre
            pred_re = vre if pred_re is None else pred_re + vre
            pred_im = vim if pred_im is None else pred_im + vim
        ere = scale_ref[:, ln] * (pred_re - vis_ref[0, at, ln].astype(F32))
        eim = scale_ref[:, ln] * (pred_im - vis_ref[1, at, ln].astype(F32))
        for f in range(facets):
            are, aim, bre, bim, mre, mim = parts(f)
            qre, qim = ere * mre + eim * mim, eim * mre - ere * mim
            values = (
                (qre * bre - qim * bim, qre * bim + qim * bre),
                (qre * are + qim * aim, qre * aim - qim * are),
            )
            for side in range(2):
                for c in range(2):
                    hi, lo = halves(values[side][c])
                    first = 2 * side * rows + lanes * width
                    grads_ref[rows_of(2 * f + c), first : first + width] = hi
                    grads_ref[rows_of(2 * f + c), first + rows : first + rows + width] = lo
            pre, pim = are * bre + aim * bim, aim * bre - are * bim
            models = (ere * pre + eim * pim, eim * pre - ere * pim)
            for c in range(2):
                n = c * facets + f
                slope = models[c] * ramp
                grad_degrid_ref[0, n, :, ln] += models[c][:8] + models[c][8:]
                grad_degrid_ref[1, n, :, ln] += slope[:8] + slope[8:]


def place_grads(grad_degrid_ref, place_ref, store_value):
    planes = grad_degrid_ref.shape[1]
    rows = grad_degrid_ref.shape[3]
    devices = place_ref.shape[1]
    odd = (iota((8, rows), 0) & 1) == 1
    full = []
    for n in range(planes):
        level = jnp.sum(grad_degrid_ref[0, n], axis=0, keepdims=True)
        slope = jnp.sum(grad_degrid_ref[1, n], axis=0, keepdims=True)
        full.append(jnp.where(odd, slope, level))
    hi, lo = halves(jnp.concatenate(full, axis=0))
    group = (iota((devices, LANES), 1) >> 1) & 3
    for h in range(2):
        value = jnp.zeros((devices, LANES), F32)
        for g in range(4):
            place = place_ref[4 * h + g]
            value = jnp.where(group == g, dot_nt(place, hi) + dot_nt(place, lo), value)
        store_value(h, value)


class Exchange:
    def __init__(self, send_ref, receive_ref, sems):
        self.send_ref, self.receive_ref, self.sems = send_ref, receive_ref, sems

    def own(self, me):
        return pltpu.make_async_copy(self.send_ref.at[me], self.receive_ref.at[me], self.sems.at[1])

    def start(self, me, groups):
        devices = self.send_ref.shape[0]
        self.own(me).start()

        @pl.loop(1, devices)
        def _(n):
            to = lax.rem(me + n, devices)
            pltpu.make_async_remote_copy(
                src_ref=self.send_ref.at[to],
                dst_ref=self.receive_ref.at[me],
                send_sem=self.sems.at[0],
                recv_sem=self.sems.at[1],
                device_id=(to // groups, lax.rem(to, groups)),
                device_id_type=pl.DeviceIdType.MESH,
            ).start()

    def wait_receive(self):
        pltpu.make_async_copy(self.receive_ref, self.receive_ref, self.sems.at[1]).wait()

    def wait_send(self):
        others = pl.ds(0, self.send_ref.shape[0] - 1)
        pltpu.make_async_copy(self.send_ref.at[others], self.send_ref.at[others], self.sems.at[0]).wait()


def main_kernel(
    owner_ref, offset_ref, taps_ref, own_ref, vis_ref, noise_ref, keep_ref, pairs_ref, sky_ref,
    words_ref, firsts_ref, grad_ref, data_ref,
    send_a, got_a, send_c, got_c, send_e, got_e, gains, send_g, got_g, near,
    place, stage, cells, weight, product, slots, part, degrid, turned, gather, sums, scale,
    left, right, grads, grad_degrid,
    sky_sem, slot_sem, sem_a, sem_c, sem_e, gain_sem, near_sem, sum_sem,
    channels, times, groups,
):
    time, group = lax.axis_index("tm"), lax.axis_index("bl")
    devices = times * groups
    me = time * groups + group
    barrier = pltpu.get_barrier_semaphore()

    @pl.loop(1, devices)
    def _(n):
        to = lax.rem(me + n, devices)
        pl.semaphore_signal(
            barrier, inc=1, device_id=(to // groups, lax.rem(to, groups)), device_id_type=pl.DeviceIdType.MESH
        )

    sky_copy = pltpu.make_async_copy(sky_ref, stage, sky_sem)
    sky_copy.start()

    def store_message(message):
        for t in range(devices):
            send_a[t] = message[t : t + 1, :]

    form_slots(owner_ref, offset_ref, taps_ref, place, store_message)
    pl.semaphore_wait(barrier, devices - 1)

    first = Exchange(send_a, got_a, sem_a)
    first.start(me, groups)

    mine = gains.at[pl.ds(group * 8, 8)]
    pltpu.make_async_copy(own_ref, mine, gain_sem.at[1]).start()

    @pl.loop(1, groups)
    def _(n):
        pltpu.make_async_remote_copy(
            src_ref=own_ref, dst_ref=mine, send_sem=gain_sem.at[0], recv_sem=gain_sem.at[1],
            device_id=(time, lax.rem(group + n, groups)), device_id_type=pl.DeviceIdType.MESH,
        ).start()

    def pass_on(n, step):
        return pltpu.make_async_remote_copy(
            src_ref=own_ref, dst_ref=near.at[n], send_sem=near_sem.at[2 * n], recv_sem=near_sem.at[2 * n + 1],
            device_id=(lax.rem(time + step, times), group), device_id_type=pl.DeviceIdType.MESH,
        )

    below, above = pass_on(0, 1), pass_on(1, times - 1)
    below.start()
    above.start()

    sky_copy.wait()
    transpose_grid(stage, cells)
    scale[...] = noise_ref[...] * keep_ref[...].astype(F32)
    station_tables(pairs_ref, gather, sums)
    grad_degrid[...] = jnp.zeros_like(grad_degrid)

    first.wait_receive()
    words_ref[...] = got_a[...].reshape(devices, LANES)
    turned_words = words_ref[...].T
    firsts = jnp.concatenate([turned_words[j * WORDS + 8 : j * WORDS + 9, :] for j in range(8)], axis=0)
    firsts_ref[...] = jnp.clip(firsts.astype(I32), 0, cells.shape[0] - 8)
    slot_copy = pltpu.make_async_copy(firsts_ref, slots, slot_sem)
    slot_copy.start()
    spread_taps(words_ref, weight)
    slot_copy.wait()

    def store_value(h, value):
        send_c[:, h, :] = value

    degrid_slots(slots, words_ref, cells, weight, product, store_value)
    second = Exchange(send_c, got_c, sem_c)
    second.start(me, groups)

    pltpu.make_async_copy(gains, gains, gain_sem.at[1]).wait()
    turn_gains(gains, turned, channels)
    gather_gains(turned, gather, left, right)

    second.wait_receive()
    gather_degrid(lambda h: got_c[:, h, :], place, part, degrid)

    @pl.loop(0, channels // CHUNK)
    def _(chunk):
        row_step(chunk, channels, vis_ref, scale, degrid, left, right, grads, grad_degrid)

    def store_grad(h, value):
        send_e[:, h, :] = value

    place_grads(grad_degrid, place, store_grad)
    third = Exchange(send_e, got_e, sem_e)
    third.start(me, groups)

    def to_peer(n, fc):
        to = lax.rem(group + n, groups)
        return pltpu.make_async_remote_copy(
            src_ref=send_g.at[fc, pl.ds(to * 8, 8)], dst_ref=got_g.at[group, fc],
            send_sem=sum_sem.at[0], recv_sem=sum_sem.at[1],
            device_id=(time, to), device_id_type=pl.DeviceIdType.MESH,
        )

    @pl.loop(0, 16)
    def _(fc):
        sums_here = dot_nt(sums[...], grads[pl.ds(pl.multiple_of(fc * channels, CHUNK), channels), :])
        send_g[fc] = jnp.concatenate([sums_here, jnp.zeros((64, 2 * LANES - channels), F32)], axis=1)
        pltpu.make_async_copy(send_g.at[fc, pl.ds(group * 8, 8)], got_g.at[group, fc], sum_sem.at[1]).start()

        @pl.loop(1, groups)
        def _(n):
            to_peer(n, fc).start()

    third.wait_receive()
    grad_ref[...] = got_e[...]
    below.wait()
    above.wait()
    pltpu.make_async_copy(got_g, got_g, sum_sem.at[1]).wait()
    for fc in range(16):
        total = got_g[0, fc]
        for n in range(1, groups):
            total = total + got_g[n, fc]
        for lt in range(2):
            here = own_ref[:, 2 * fc + lt, :]
            down = jnp.where(time > 0, here - near[0, :, 2 * fc + lt, :], 0.0)
            up = jnp.where(time < times - 1, near[1, :, 2 * fc + lt, :] - here, 0.0)
            data_ref[fc, :, lt * LANES : (lt + 1) * LANES] = (
                total[:, lt * LANES : (lt + 1) * LANES] + smoothness * (down - up)
            )

    first.wait_send()
    second.wait_send()
    third.wait_send()
    others = gains.at[pl.ds(0, 8 * (groups - 1))]
    pltpu.make_async_copy(others, others, gain_sem.at[0]).wait()
    sent = got_g.at[pl.ds(0, groups - 1)]
    pltpu.make_async_copy(sent, sent, sum_sem.at[0]).wait()


def scatter_kernel(first_ref, words_ref, grad_ref, sky_ref, weight_ref, spread, cells, stage, sem):
    sources = grad_ref.shape[0]
    blocks = stage.shape[1] // 8
    for b in range(blocks):
        cells[b * STRIDE : (b + 1) * STRIDE, :] = jnp.zeros((STRIDE, LANES), F32)
    spread_taps(words_ref, weight_ref)
    fold = fold_table()
    lane_quarter = (iota((sources, LANES), 1) >> 1) & 3
    for h in range(2):
        block = grad_ref[:, h, :]
        for g in range(4):
            j = 4 * h + g
            part = jnp.concatenate(halves(jnp.where(lane_quarter == g, block, 0.0)), axis=1)
            spread[j] = jnp.where(slot_quarter(words_ref, j) == lane_quarter.astype(F32), dot(part, fold), 0.0)

    @pl.loop(0, sources, unroll=2)
    def _(s):
        at = pl.ds(pl.multiple_of(s * 8, 8), 8)
        for j in range(8):
            cells[pl.ds(first_ref[j, s], 8), :] += weight_ref[j, at, :] * spread[j, pl.ds(s, 1), :]

    quarter = (iota((8, LANES), 1) >> 1) & 3
    last = jnp.zeros((8, LANES), F32)
    for b in range(blocks):
        pads = cells[b * STRIDE + LANES : (b + 1) * STRIDE, :]
        head = slice(b * STRIDE, b * STRIDE + 8)
        cells[head, :] = cells[head, :] + jnp.where(quarter > 0, pltpu.roll(pads, 2, 1), last)
        last = pltpu.roll(pads, LANES - 6, 1)

    pieces = 4
    length = blocks // pieces

    def copy(n):
        at = pl.ds(n * length * 8, length * 8)
        return pltpu.make_async_copy(stage.at[:, at, :], sky_ref.at[:, at, :], sem.at[n])

    for n in range(pieces):

        @pl.loop(n * length, (n + 1) * length, unroll=8)
        def _(b):
            turned = cells[pl.ds(pl.multiple_of(b * STRIDE, 8), LANES), :].T
            stage[:, pl.ds(pl.multiple_of(b * 8, 8), 8), :] = turned.reshape(16, 8, LANES)

        copy(n).start()
    for n in range(pieces):
        copy(n).wait()


def vmem(count):
    return [pl.BlockSpec(memory_space=pltpu.VMEM)] * count


def shape(dims, dtype=F32):
    return jax.ShapeDtypeStruct(dims, dtype)


def params():
    return pltpu.CompilerParams(vmem_limit_bytes=VMEM_LIMIT)


def body(
    visibilities, noise_weight, keep_flag, station_pairs, tile_owner, tile_offset, kernel_taps, gain_field, sky_grid
):
    rows = visibilities.shape[0]
    channels = visibilities.shape[2]
    devices = lax.axis_size("tm") * lax.axis_size("bl")
    parts, facets, terms, cells = sky_grid.shape
    lines = cells // LANES
    sky = sky_grid.reshape(parts, facets, terms, lines, LANES).transpose(0, 1, 3, 2, 4)
    sky = sky.reshape(parts * facets, lines * terms, LANES)

    own = jnp.pad(gain_field[0], ((0, 0), (0, 0), (0, 0), (0, 2 * LANES - channels)))
    own = own.reshape(-1, facets * 4, LANES)
    pieces = pltpu.VMEM((devices, 2, LANES), F32)
    words, firsts, grad, data = pl.pallas_call(
        functools.partial(
            main_kernel, channels=channels, times=lax.axis_size("tm"), groups=lax.axis_size("bl")
        ),
        out_shape=(
            shape((devices, LANES)), shape((8, devices), I32), shape((devices, 2, LANES)),
            shape((2 * facets, 8, 2 * LANES)),
        ),
        in_specs=vmem(8) + [pl.BlockSpec(memory_space=pl.ANY)],
        out_specs=tuple(vmem(4)),
        scratch_shapes=[
            pltpu.VMEM((devices, 1, LANES), F32),
            pltpu.VMEM((devices, 1, LANES), F32),
            pieces,
            pieces,
            pieces,
            pieces,
            pltpu.VMEM((64, facets * 4, LANES), F32),
            pltpu.VMEM((2 * facets, 64, 2 * LANES), F32),
            pltpu.VMEM((8, 2 * facets, 8, 2 * LANES), F32),
            pltpu.VMEM((2, 8, facets * 4, LANES), F32),
            pltpu.VMEM((8, devices, rows), BF16),
            pltpu.VMEM(sky.shape, F32),
            pltpu.VMEM((cells // BLOCK * STRIDE, LANES), F32),
            pltpu.VMEM((8, devices * 8, LANES), F32),
            pltpu.VMEM((8, devices * 8, LANES), F32),
            pltpu.SMEM((8, devices), I32),
            pltpu.VMEM((rows // LANES, LANES, LANES), F32),
            pltpu.VMEM((2, 16, rows), F32),
            pltpu.VMEM((2 * facets * channels, LANES), BF16),
            pltpu.VMEM((2, LANES, rows), BF16),
            pltpu.VMEM((64, 4 * rows), BF16),
            pltpu.VMEM((1, rows), F32),
            pltpu.VMEM((2 * facets * channels, rows), F32),
            pltpu.VMEM((2 * facets * channels, rows), F32),
            pltpu.VMEM((2 * facets * channels, 4 * rows), BF16),
            pltpu.VMEM((2, 2 * facets, 8, rows), F32),
            pltpu.SemaphoreType.DMA,
            pltpu.SemaphoreType.DMA,
            pltpu.SemaphoreType.DMA((2,)),
            pltpu.SemaphoreType.DMA((2,)),
            pltpu.SemaphoreType.DMA((2,)),
            pltpu.SemaphoreType.DMA((2,)),
            pltpu.SemaphoreType.DMA((4,)),
            pltpu.SemaphoreType.DMA((2,)),
        ],
        compiler_params=pltpu.CompilerParams(
            vmem_limit_bytes=62 << 20, collective_id=0, has_side_effects=True
        ),
        name="main",
    )(
        tile_owner.reshape(1, rows), tile_offset.reshape(1, rows), kernel_taps, own,
        visibilities.transpose(1, 2, 0), noise_weight.reshape(1, rows), keep_flag.reshape(1, rows),
        station_pairs, sky,
    )

    out_grid = pl.pallas_call(
        scatter_kernel,
        out_shape=shape(sky.shape),
        in_specs=[pl.BlockSpec(memory_space=pltpu.SMEM)] + vmem(2),
        out_specs=pl.BlockSpec(memory_space=pl.ANY),
        scratch_shapes=[
            pltpu.VMEM((8, devices * 8, LANES), F32),
            pltpu.VMEM((8, devices, LANES), F32),
            pltpu.VMEM((cells // BLOCK * STRIDE, LANES), F32),
            pltpu.VMEM(sky.shape, F32),
            pltpu.SemaphoreType.DMA((4,)),
        ],
        compiler_params=params(),
        name="scatter",
    )(firsts, words, grad)
    grid_gradient = out_grid.reshape(parts, facets, lines, terms, LANES).transpose(0, 1, 3, 2, 4)
    grid_gradient = grid_gradient.reshape(sky_grid.shape)

    data = data.reshape(facets, 2, 8, 2 * LANES).transpose(2, 0, 1, 3)[None, :, :, :, :channels]
    return (data, grid_gradient)


def solution(mesh):
    split = ("tm", "bl")
    return jax.shard_map(
        body,
        mesh=mesh,
        in_specs=(
            P(split, None, None),
            P(split),
            P(split),
            P(None, split),
            P(split, None),
            P(split),
            P(None, split),
            P("tm", "bl", None, None, None),
            P(None, None, None, split),
        ),
        out_specs=(P("tm", "bl", None, None, None), P(None, None, None, split)),
        check_vma=False,
    )
```

time: 138 us -> 77.7 us (0.56)
  blocking collectives: 36.6 us -> 0 us
  between operations: 14.1 us -> 0.65 us
  starting transfers between devices: 9.19 us -> 0 us
  Pallas kernels: 68 us -> 73.5 us
  waiting for transfers between devices: 5.19 us -> 0 us
  other arithmetic: 1.43 us -> 0 us
    all_to_all x2 -> x0, blocking collectives: 36.6 us -> none  [the longest x1 20.8 us: body(): lax.all_to_all(message, ('tm', 'bl'), split_axis=0, concat_axis=0, tiled=...]
    pallas_call x3 -> x1, Pallas kernels: 47.8 us -> 63.4 us  [body(): pl.pallas_call(functools.partial(main_kernel, channels=channels, times=la...]
    pallas_call x1, Pallas kernels: 20.3 us -> 10.1 us  [body(): pl.pallas_call(scatter_kernel, out_shape=shape(sky.shape), in_specs=[pl.B...]
    all_to_all x1 -> x0, waiting for transfers between devices: 5.13 us -> none  [body(): lax.all_to_all(grad, ('tm', 'bl'), split_axis=0, concat_axis=0, tiled=True)]
    ppermute x2 -> x0, starting transfers between devices: 4.59 us -> none  [the longest x1 3.3 us: body(): lax.ppermute(gain_field, 'tm', [(i, i + 1) for i in range(times - 1)])]
    all_to_all x1 -> x0, starting transfers between devices: 4.52 us -> none  [body(): lax.all_to_all(grad, ('tm', 'bl'), split_axis=0, concat_axis=0, tiled=True)]
  transfers between devices with their start and end apart: 5 -> 0, of which waited for: 1 -> 0; matrix products, arithmetic and copies ran while one was open for 1% -> 0% of each run, Pallas kernels for 33% -> 0%
where the time goes in v2:
time: 77.7 us; the launch traced here: 77.5 us
  Pallas kernels  73.5 us (95%)
  local copies, waits for them, and re-layouts  3.35 us (4%)
    pallas_call x1, Pallas kernels, body(): pl.pallas_call(functools.partial(main_kernel, channels=channels, times=la...  63.4 us
    pallas_call x1, Pallas kernels, body(): pl.pallas_call(scatter_kernel, out_shape=shape(sky.shape), in_specs=[pl.B...  10.1 us

profile of v2, /device:TPU:1, one launch (start us, length us, event | category | flops | bytes accessed | tf_op | source)
XLA Modules:
  0.0 77.5 jit_solution(17208955289826455323)
XLA Ops:
  0.6 1.0 %pad.4 = f32[8,8,2,256]{3,2,1,0:T(2,128)S(1)} pad(f32[8,8,2,240]{3,2,1,0:T(2,128)} %bitcast.26, f32[]{:T(128)} %constant.2.clone.1), padding=0_0x0_0x0_0x0_16 | pad | bytes 253956 | tf_op jit(solution)/shard_map/jit(_pad)/pad | solution.py:486
  1.6 0.8 reshape.36.own_ref
  2.3 63.4 %main.1 = (f32[128,128]{1,0:T(8,128)}, s32[8,128]{1,0:T(8,128)}, f32[128,2,128]{2,1,0:T(2,128)}, f32[16,8,256]{2,1,0:T(8,128)}) custom-call(s32[1,512]{1,0:T(1,128)} %bitcast.28, s32[1,512]{1,0:T(1,128)} %bitcast.29, f32[8,512]{1,0:T(8,128)} %taps_ref.1, f32[8,32,128]{2,1,0:T(8,128)} %reshape.36.own_ref, bf16[2,240,512]{2,1,0:T(8,128)(2,1)} %bitcast.25, ...), custom_call_target="tpu_custom_call" | custom-call | tf_op jit(solution)/shard_map/main/pallas_call | solution.py:489
  65.8 1.0 %copy.15 = f32[8,2,8,256]{3,1,0,2:T(2,128)S(1)} copy(f32[8,2,8,256]{3,2,1,0:T(8,128)} %bitcast.27) | data formatting | bytes 262144 | tf_op jit(solution)/shard_map/reshape | solution.py:563
  66.8 0.7 slice_bitcast_fusion
  67.4 10.1 %scatter.1 = f32[16,512,128]{2,1,0:T(8,128)} custom-call(s32[8,128]{1,0:T(8,128)} %get-tuple-element.7.first_ref, f32[128,128]{1,0:T(8,128)} %get-tuple-element.8.words_ref, f32[128,2,128]{2,1,0:T(2,128)} %get-tuple-element.9.grad_ref), custom_call_target="tpu_custom_call" | custom-call | tf_op jit(solution)/shard_map/scatter/pallas_call | solution.py:545

commit v3 on v2

--- a/solution.py
+++ b/solution.py
@@ -153,7 +153,7 @@
     for fc in range(16):
         tiles = []
         for lt in range(2):
-            block = gains_ref[:, 2 * fc + lt, :]
+            block = gains_ref[:, :, :, 2 * fc + lt, :].reshape(64, LANES)
             hi = block.astype(BF16).astype(F32)
             tiles.append(jnp.concatenate([hi, block - hi], axis=0).T)
         turned_ref[fc * channels : (fc + 1) * channels] = jnp.concatenate(tiles, axis=0)[:channels].astype(BF16)
@@ -243,92 +243,116 @@
 
 
 class Exchange:
-    def __init__(self, send_ref, receive_ref, sems):
-        self.send_ref, self.receive_ref, self.sems = send_ref, receive_ref, sems
-
-    def own(self, me):
-        return pltpu.make_async_copy(self.send_ref.at[me], self.receive_ref.at[me], self.sems.at[1])
-
-    def start(self, me, groups):
-        devices = self.send_ref.shape[0]
-        self.own(me).start()
-
-        @pl.loop(1, devices)
+    def __init__(self, send_ref, middle_ref, receive_ref, sems, time, group):
+        self.send_ref, self.middle_ref, self.receive_ref, self.sems = send_ref, middle_ref, receive_ref, sems
+        self.time, self.group = time, group
+        self.times, self.groups = send_ref.shape[:2]
+
+    def start(self):
+        to_middle = self.middle_ref.at[:, self.time]
+        pltpu.make_async_copy(self.send_ref.at[self.time], to_middle, self.sems.at[1]).start()
+
+        @pl.loop(1, self.times)
         def _(n):
-            to = lax.rem(me + n, devices)
-            pltpu.make_async_remote_copy(
-                src_ref=self.send_ref.at[to],
-                dst_ref=self.receive_ref.at[me],
-                send_sem=self.sems.at[0],
-                recv_sem=self.sems.at[1],
-                device_id=(to // groups, lax.rem(to, groups)),
-                device_id_type=pl.DeviceIdType.MESH,
-            ).start()
+            to = lax.rem(self.time + n, self.times)
+            remote(self.send_ref.at[to], to_middle, self.sems.at[0], self.sems.at[1], (to, self.group)).start()
+
+    def pass_on(self):
+        wait_bytes(self.middle_ref, self.sems.at[1])
+        to_end = self.receive_ref.at[:, self.group]
+        pltpu.make_async_copy(self.middle_ref.at[self.group], to_end, self.sems.at[3]).start()
+
+        @pl.loop(1, self.groups)
+        def _(n):
+            to = lax.rem(self.group + n, self.groups)
+            remote(self.middle_ref.at[to], to_end, self.sems.at[2], self.sems.at[3], (self.time, to)).start()
 
     def wait_receive(self):
-        pltpu.make_async_copy(self.receive_ref, self.receive_ref, self.sems.at[1]).wait()
+        wait_bytes(self.receive_ref, self.sems.at[3])
 
     def wait_send(self):
-        others = pl.ds(0, self.send_ref.shape[0] - 1)
-        pltpu.make_async_copy(self.send_ref.at[others], self.send_ref.at[others], self.sems.at[0]).wait()
+        wait_bytes(self.send_ref.at[pl.ds(0, self.times - 1)], self.sems.at[0])
+        wait_bytes(self.middle_ref.at[pl.ds(0, self.groups - 1)], self.sems.at[2])
+
+
+def remote(source, target, send_sem, receive_sem, device):
+    return pltpu.make_async_remote_copy(
+        src_ref=source, dst_ref=target, send_sem=send_sem, recv_sem=receive_sem,
+        device_id=device, device_id_type=pl.DeviceIdType.MESH,
+    )
+
+
+def wait_bytes(ref, sem):
+    pltpu.make_async_copy(ref, ref, sem).wait()
 
 
 def main_kernel(
-    owner_ref, offset_ref, taps_ref, own_ref, vis_ref, noise_ref, keep_ref, pairs_ref, sky_ref,
+    owner_ref, offset_ref, taps_ref, gain_ref, vis_ref, noise_ref, keep_ref, pairs_ref, sky_ref,
     words_ref, firsts_ref, grad_ref, data_ref,
-    send_a, got_a, send_c, got_c, send_e, got_e, gains, send_g, got_g, near,
+    send_a, mid_a, got_a, send_c, mid_c, got_c, send_e, mid_e, got_e, own, gains, send_g, got_g, near,
     place, stage, cells, weight, product, slots, part, degrid, turned, gather, sums, scale,
     left, right, grads, grad_degrid,
-    sky_sem, slot_sem, sem_a, sem_c, sem_e, gain_sem, near_sem, sum_sem,
+    sky_sem, slot_sem, sem_a, sem_c, sem_e, gain_sem, pair_sem, near_sem, sum_sem,
     channels, times, groups,
 ):
     time, group = lax.axis_index("tm"), lax.axis_index("bl")
     devices = times * groups
-    me = time * groups + group
+    level, core = group // 2, lax.rem(group, 2)
+    facets = gain_ref.shape[1]
     barrier = pltpu.get_barrier_semaphore()
 
-    @pl.loop(1, devices)
+    @pl.loop(1, times)
     def _(n):
-        to = lax.rem(me + n, devices)
-        pl.semaphore_signal(
-            barrier, inc=1, device_id=(to // groups, lax.rem(to, groups)), device_id_type=pl.DeviceIdType.MESH
-        )
+        to = (lax.rem(time + n, times), group)
+        pl.semaphore_signal(barrier, inc=1, device_id=to, device_id_type=pl.DeviceIdType.MESH)
+
+    @pl.loop(1, groups)
+    def _(n):
+        to = (time, lax.rem(group + n, groups))
+        pl.semaphore_signal(barrier, inc=1, device_id=to, device_id_type=pl.DeviceIdType.MESH)
 
     sky_copy = pltpu.make_async_copy(sky_ref, stage, sky_sem)
     sky_copy.start()
 
     def store_message(message):
         for t in range(devices):
-            send_a[t] = message[t : t + 1, :]
+            send_a[t // groups, t % groups] = message[t : t + 1, :]
 
     form_slots(owner_ref, offset_ref, taps_ref, place, store_message)
-    pl.semaphore_wait(barrier, devices - 1)
-
-    first = Exchange(send_a, got_a, sem_a)
-    first.start(me, groups)
-
-    mine = gains.at[pl.ds(group * 8, 8)]
-    pltpu.make_async_copy(own_ref, mine, gain_sem.at[1]).start()
-
-    @pl.loop(1, groups)
+    pl.semaphore_wait(barrier, times + groups - 2)
+
+    first = Exchange(send_a, mid_a, got_a, sem_a, time, group)
+    second = Exchange(send_c, mid_c, got_c, sem_c, time, group)
+    third = Exchange(send_e, mid_e, got_e, sem_e, time, group)
+    first.start()
+
+    for f in range(facets):
+        for c in range(2):
+            for lt in range(2):
+                wide = min(LANES, channels - lt * LANES)
+                block = gain_ref[:, f, c, lt * LANES : lt * LANES + wide]
+                if wide < LANES:
+                    block = jnp.concatenate([block, jnp.zeros((block.shape[0], LANES - wide), F32)], axis=1)
+                own[:, 4 * f + 2 * c + lt, :] = block
+    mine = gains.at[level, core]
+    pltpu.make_async_copy(own, mine, gain_sem.at[1]).start()
+
+    @pl.loop(1, groups // 2)
     def _(n):
-        pltpu.make_async_remote_copy(
-            src_ref=own_ref, dst_ref=mine, send_sem=gain_sem.at[0], recv_sem=gain_sem.at[1],
-            device_id=(time, lax.rem(group + n, groups)), device_id_type=pl.DeviceIdType.MESH,
-        ).start()
-
-    def pass_on(n, step):
-        return pltpu.make_async_remote_copy(
-            src_ref=own_ref, dst_ref=near.at[n], send_sem=near_sem.at[2 * n], recv_sem=near_sem.at[2 * n + 1],
-            device_id=(lax.rem(time + step, times), group), device_id_type=pl.DeviceIdType.MESH,
-        )
-
-    below, above = pass_on(0, 1), pass_on(1, times - 1)
+        to = lax.rem(group + 2 * n, groups)
+        remote(own, mine, gain_sem.at[0], gain_sem.at[1], (time, to)).start()
+
+    def next_interval(n, step):
+        to = lax.rem(time + step, times)
+        return remote(own, near.at[n], near_sem.at[2 * n], near_sem.at[2 * n + 1], (to, group))
+
+    below, above = next_interval(0, 1), next_interval(1, times - 1)
     below.start()
     above.start()
 
     sky_copy.wait()
     transpose_grid(stage, cells)
+    first.pass_on()
     scale[...] = noise_ref[...] * keep_ref[...].astype(F32)
     station_tables(pairs_ref, gather, sums)
     grad_degrid[...] = jnp.zeros_like(grad_degrid)
@@ -344,72 +368,80 @@
     slot_copy.wait()
 
     def store_value(h, value):
-        send_c[:, h, :] = value
+        send_c[:, :, h, :] = value.reshape(times, groups, LANES)
 
     degrid_slots(slots, words_ref, cells, weight, product, store_value)
-    second = Exchange(send_c, got_c, sem_c)
-    second.start(me, groups)
-
-    pltpu.make_async_copy(gains, gains, gain_sem.at[1]).wait()
+    second.start()
+
+    column = gains.at[:, core]
+    wait_bytes(column, gain_sem.at[1])
+    to_pair = remote(column, column, pair_sem.at[0], pair_sem.at[1], (time, group + 1 - 2 * core))
+    to_pair.start()
+    second.pass_on()
+    wait_bytes(column, pair_sem.at[1])
     turn_gains(gains, turned, channels)
     gather_gains(turned, gather, left, right)
 
     second.wait_receive()
-    gather_degrid(lambda h: got_c[:, h, :], place, part, degrid)
+    gather_degrid(lambda h: got_c[:, :, h, :].reshape(devices, LANES), place, part, degrid)
 
     @pl.loop(0, channels // CHUNK)
     def _(chunk):
         row_step(chunk, channels, vis_ref, scale, degrid, left, right, grads, grad_degrid)
 
     def store_grad(h, value):
-        send_e[:, h, :] = value
+        send_e[:, :, h, :] = value.reshape(times, groups, LANES)
 
     place_grads(grad_degrid, place, store_grad)
-    third = Exchange(send_e, got_e, sem_e)
-    third.start(me, groups)
-
-    def to_peer(n, fc):
-        to = lax.rem(group + n, groups)
-        return pltpu.make_async_remote_copy(
-            src_ref=send_g.at[fc, pl.ds(to * 8, 8)], dst_ref=got_g.at[group, fc],
-            send_sem=sum_sem.at[0], recv_sem=sum_sem.at[1],
-            device_id=(time, to), device_id_type=pl.DeviceIdType.MESH,
-        )
-
-    @pl.loop(0, 16)
-    def _(fc):
-        sums_here = dot_nt(sums[...], grads[pl.ds(pl.multiple_of(fc * channels, CHUNK), channels), :])
-        send_g[fc] = jnp.concatenate([sums_here, jnp.zeros((64, 2 * LANES - channels), F32)], axis=1)
-        pltpu.make_async_copy(send_g.at[fc, pl.ds(group * 8, 8)], got_g.at[group, fc], sum_sem.at[1]).start()
+    third.start()
+
+    batch = 4
+
+    def sum_batch(b):
+        for i in range(batch):
+            fc = b * batch + i
+            value = dot_nt(sums[...], grads[fc * channels : (fc + 1) * channels, :])
+            send_g[fc] = jnp.concatenate([value, jnp.zeros((64, 2 * LANES - channels), F32)], axis=1)
+        these = pl.ds(b * batch, batch)
+        to_end = got_g.at[group, these]
+        pltpu.make_async_copy(send_g.at[these, pl.ds(group * 8, 8)], to_end, sum_sem.at[1]).start()
 
         @pl.loop(1, groups)
         def _(n):
-            to_peer(n, fc).start()
+            to = lax.rem(group + n, groups)
+            remote(send_g.at[these, pl.ds(to * 8, 8)], to_end, sum_sem.at[0], sum_sem.at[1], (time, to)).start()
+
+    sum_batch(0)
+    third.pass_on()
+    for b in range(1, 2 * facets // batch):
+        sum_batch(b)
 
     third.wait_receive()
-    grad_ref[...] = got_e[...]
+    grad_ref[...] = got_e[...].reshape(devices, 2, LANES)
     below.wait()
     above.wait()
-    pltpu.make_async_copy(got_g, got_g, sum_sem.at[1]).wait()
-    for fc in range(16):
-        total = got_g[0, fc]
-        for n in range(1, groups):
-            total = total + got_g[n, fc]
-        for lt in range(2):
-            here = own_ref[:, 2 * fc + lt, :]
-            down = jnp.where(time > 0, here - near[0, :, 2 * fc + lt, :], 0.0)
-            up = jnp.where(time < times - 1, near[1, :, 2 * fc + lt, :] - here, 0.0)
-            data_ref[fc, :, lt * LANES : (lt + 1) * LANES] = (
-                total[:, lt * LANES : (lt + 1) * LANES] + smoothness * (down - up)
-            )
+    wait_bytes(got_g, sum_sem.at[1])
+    for f in range(facets):
+        for c in range(2):
+            fc = 2 * f + c
+            total = got_g[0, fc]
+            for n in range(1, groups):
+                total = total + got_g[n, fc]
+            smooth = []
+            for lt in range(2):
+                here = own[:, 2 * fc + lt, :]
+                down = jnp.where(time > 0, here - near[0, :, 2 * fc + lt, :], 0.0)
+                up = jnp.where(time < times - 1, near[1, :, 2 * fc + lt, :] - here, 0.0)
+                smooth.append(down - up)
+            total = total + smoothness * jnp.concatenate(smooth, axis=1)
+            data_ref[:, f, c, :] = total[:, :channels]
 
     first.wait_send()
     second.wait_send()
     third.wait_send()
-    others = gains.at[pl.ds(0, 8 * (groups - 1))]
-    pltpu.make_async_copy(others, others, gain_sem.at[0]).wait()
-    sent = got_g.at[pl.ds(0, groups - 1)]
-    pltpu.make_async_copy(sent, sent, sum_sem.at[0]).wait()
+    wait_bytes(gains.at[pl.ds(0, groups // 2 - 1), 0], gain_sem.at[0])
+    wait_bytes(column, pair_sem.at[0])
+    wait_bytes(got_g.at[pl.ds(0, groups - 1)], sum_sem.at[0])
 
 
 def scatter_kernel(first_ref, words_ref, grad_ref, sky_ref, weight_ref, spread, cells, stage, sem):
@@ -483,30 +515,30 @@
     sky = sky_grid.reshape(parts, facets, terms, lines, LANES).transpose(0, 1, 3, 2, 4)
     sky = sky.reshape(parts * facets, lines * terms, LANES)
 
-    own = jnp.pad(gain_field[0], ((0, 0), (0, 0), (0, 0), (0, 2 * LANES - channels)))
-    own = own.reshape(-1, facets * 4, LANES)
-    pieces = pltpu.VMEM((devices, 2, LANES), F32)
+    times, groups = lax.axis_size("tm"), lax.axis_size("bl")
+    singles, pairs = pltpu.VMEM((times, groups, 1, LANES), F32), pltpu.VMEM((times, groups, 2, LANES), F32)
+    middle_singles = pltpu.VMEM((groups, times, 1, LANES), F32)
+    middle_pairs = pltpu.VMEM((groups, times, 2, LANES), F32)
+    tiles = facets * 4
     words, firsts, grad, data = pl.pallas_call(
         functools.partial(
-            main_kernel, channels=channels, times=lax.axis_size("tm"), groups=lax.axis_size("bl")
+            main_kernel, channels=channels, times=times, groups=groups
         ),
         out_shape=(
             shape((devices, LANES)), shape((8, devices), I32), shape((devices, 2, LANES)),
-            shape((2 * facets, 8, 2 * LANES)),
+            shape(gain_field.shape[1:]),
         ),
         in_specs=vmem(8) + [pl.BlockSpec(memory_space=pl.ANY)],
         out_specs=tuple(vmem(4)),
         scratch_shapes=[
-            pltpu.VMEM((devices, 1, LANES), F32),
-            pltpu.VMEM((devices, 1, LANES), F32),
-            pieces,
-            pieces,
-            pieces,
-            pieces,
-            pltpu.VMEM((64, facets * 4, LANES), F32),
+            singles, middle_singles, singles,
+            pairs, middle_pairs, pairs,
+            pairs, middle_pairs, pairs,
+            pltpu.VMEM((8, tiles, LANES), F32),
+            pltpu.VMEM((groups // 2, 2, 8, tiles, LANES), F32),
             pltpu.VMEM((2 * facets, 64, 2 * LANES), F32),
-            pltpu.VMEM((8, 2 * facets, 8, 2 * LANES), F32),
-            pltpu.VMEM((2, 8, facets * 4, LANES), F32),
+            pltpu.VMEM((groups, 2 * facets, 8, 2 * LANES), F32),
+            pltpu.VMEM((2, 8, tiles, LANES), F32),
             pltpu.VMEM((8, devices, rows), BF16),
             pltpu.VMEM(sky.shape, F32),
             pltpu.VMEM((cells // BLOCK * STRIDE, LANES), F32),
@@ -525,8 +557,9 @@
             pltpu.VMEM((2, 2 * facets, 8, rows), F32),
             pltpu.SemaphoreType.DMA,
             pltpu.SemaphoreType.DMA,
-            pltpu.SemaphoreType.DMA((2,)),
-            pltpu.SemaphoreType.DMA((2,)),
+            pltpu.SemaphoreType.DMA((4,)),
+            pltpu.SemaphoreType.DMA((4,)),
+            pltpu.SemaphoreType.DMA((4,)),
             pltpu.SemaphoreType.DMA((2,)),
             pltpu.SemaphoreType.DMA((2,)),
             pltpu.SemaphoreType.DMA((4,)),
@@ -537,7 +570,7 @@
         ),
         name="main",
     )(
-        tile_owner.reshape(1, rows), tile_offset.reshape(1, rows), kernel_taps, own,
+        tile_owner.reshape(1, rows), tile_offset.reshape(1, rows), kernel_taps, gain_field[0],
         visibilities.transpose(1, 2, 0), noise_weight.reshape(1, rows), keep_flag.reshape(1, rows),
         station_pairs, sky,
     )
@@ -560,8 +593,7 @@
     grid_gradient = out_grid.reshape(parts, facets, lines, terms, LANES).transpose(0, 1, 3, 2, 4)
     grid_gradient = grid_gradient.reshape(sky_grid.shape)
 
-    data = data.reshape(facets, 2, 8, 2 * LANES).transpose(2, 0, 1, 3)[None, :, :, :, :channels]
-    return (data, grid_gradient)
+    return (data[None], grid_gradient)
 
 
 def solution(mesh):

time: 77.7 us -> 72.3 us (0.931)
  Pallas kernels: 73.5 us -> 70.5 us
  local copies, waits for them, and re-layouts: 3.35 us -> 0.66 us
    reshape x2 -> x0, local copies, waits for them, and re-layouts: 1.73 us -> none  [the longest x1 0.97 us: body(): data.reshape(facets, 2, 8, 2 * LANES).transpose(2, 0, 1, 3)]
    pallas_call x1, Pallas kernels: 63.4 us -> 61.8 us  [body(): pl.pallas_call(functools.partial(main_kernel, channels=channels, times=ti...]
    pallas_call x1, Pallas kernels: 10.1 us -> 8.67 us  [body(): pl.pallas_call(scatter_kernel, out_shape=shape(sky.shape), in_specs=[pl.B...]
    pad x1 -> x0, local copies, waits for them, and re-layouts: 0.95 us -> none  [body(): jnp.pad(gain_field[0], ((0, 0), (0, 0), (0, 0), (0, 2 * LANES - channels)))]
where the time goes in v3:
time: 72.3 us; the launch traced here: 71.8 us
  Pallas kernels  70.5 us (98%)
    pallas_call x1, Pallas kernels, body(): pl.pallas_call(functools.partial(main_kernel, channels=channels, times=ti...  61.8 us
    pallas_call x1, Pallas kernels, body(): pl.pallas_call(scatter_kernel, out_shape=shape(sky.shape), in_specs=[pl.B...  8.67 us

profile of v3, /device:TPU:1, one launch (start us, length us, event | category | flops | bytes accessed | tf_op | source)
XLA Modules:
  0.0 71.8 jit_solution(17680502746710549707)
XLA Ops:
  0.6 61.8 %main.1 = (f32[128,128]{1,0:T(8,128)}, s32[8,128]{1,0:T(8,128)}, f32[128,2,128]{2,1,0:T(2,128)}, f32[8,8,2,240]{3,2,1,0:T(2,128)}) custom-call(s32[1,512]{1,0:T(1,128)} %bitcast.22, s32[1,512]{1,0:T(1,128)} %bitcast.23, f32[8,512]{1,0:T(8,128)} %taps_ref.1, f32[8,8,2,240]{3,2,1,0:T(2,128)} %bitcast.20, bf16[2,240,512]{2,1,0:T(8,128)(2,1)} %bitcast.19, ...), custom_call_target="tpu_custom_call" | custom-call | tf_op jit(solution)/shard_map/main/pallas_call | solution.py:523
  62.4 0.0 copy-start
  62.4 8.7 %scatter.1 = f32[16,512,128]{2,1,0:T(8,128)} custom-call(s32[8,128]{1,0:T(8,128)} %get-tuple-element.7.first_ref, f32[128,128]{1,0:T(8,128)} %get-tuple-element.8.words_ref, f32[128,2,128]{2,1,0:T(2,128)} %get-tuple-element.9.grad_ref), custom_call_target="tpu_custom_call" | custom-call | tf_op jit(solution)/shard_map/scatter/pallas_call | solution.py:578
  71.1 0.0 copy-done
  71.1 0.7 copy.14
Async XLA Ops:
  62.4 8.7 %copy-start = (f32[8,8,2,240]{3,2,1,0:T(2,128)S(1)}, f32[8,8,2,240]{3,2,1,0:T(2,128)}, u32[]{:S(2)}) copy-start(f32[8,8,2,240]{3,2,1,0:T(2,128)} %get-tuple-element.6) | copy-start | bytes 368644

commit v4 on v3

--- a/solution.py
+++ b/solution.py
@@ -159,10 +159,10 @@
         turned_ref[fc * channels : (fc + 1) * channels] = jnp.concatenate(tiles, axis=0)[:channels].astype(BF16)
 
 
-def gather_gains(turned_ref, gather_ref, left_ref, right_ref):
+def gather_gains(turned_ref, gather_ref, left_ref, right_ref, first, last):
     size = turned_ref.shape[0] // 3
 
-    @pl.loop(0, 3)
+    @pl.loop(first, last)
     def _(n):
         at = pl.ds(pl.multiple_of(n * size, CHUNK), size)
         gains = turned_ref[at, :]
@@ -170,56 +170,74 @@
         right_ref[at, :] = dot(gains, gather_ref[1])
 
 
-def row_step(chunk, channels, vis_ref, scale_ref, degrid_ref, left_ref, right_ref, grads_ref, grad_degrid_ref):
+def chunk_rows(plane, channels, chunk):
+    return pl.ds(pl.multiple_of(plane * channels + chunk * CHUNK, CHUNK), CHUNK)
+
+
+def channel_ramp(channels, chunk, width):
+    channel = (iota((CHUNK, width), 0) + chunk * CHUNK).astype(F32)
+    return 2.0 * channel / (channels - 1) - 1.0
+
+
+def facet_model(degrid_ref, f, lanes, ramp):
+    g = degrid_ref.shape[1] // 2 + f
+    return tuple(degrid_ref[0, n : n + 1, lanes] + degrid_ref[1, n : n + 1, lanes] * ramp for n in (f, g))
+
+
+def error_step(
+    chunk, channels, vis_ref, scale_ref, degrid_ref, left_ref, right_ref, error_ref, grad_degrid_ref, width=LANES
+):
     rows = vis_ref.shape[2]
-    facets = left_ref.shape[0] // channels // 2
-    width = 2 * LANES
-
-    def rows_of(n):
-        return pl.ds(pl.multiple_of(n * channels + chunk * CHUNK, CHUNK), CHUNK)
-
-    at = rows_of(0)
-    channel = (iota((CHUNK, width), 0) + chunk * CHUNK).astype(F32)
-    ramp = 2.0 * channel / (channels - 1) - 1.0
-    for lanes in range(rows // width):
-        ln = slice(lanes * width, (lanes + 1) * width)
-
-        def parts(f):
-            re, im = rows_of(2 * f), rows_of(2 * f + 1)
-            g = facets + f
-            mre = degrid_ref[0, f : f + 1, ln] + degrid_ref[1, f : f + 1, ln] * ramp
-            mim = degrid_ref[0, g : g + 1, ln] + degrid_ref[1, g : g + 1, ln] * ramp
-            return left_ref[re, ln], left_ref[im, ln], right_ref[re, ln], right_ref[im, ln], mre, mim
-
-        pred_re = pred_im = None
+    facets = degrid_ref.shape[1] // 2
+    at = chunk_rows(0, channels, chunk)
+    ramp = channel_ramp(channels, chunk, width)
+    for first in range(0, rows, width):
+        lanes = slice(first, first + width)
+        products, pred_re, pred_im = [], None, None
         for f in range(facets):
-            are, aim, bre, bim, mre, mim = parts(f)
+            re, im = chunk_rows(2 * f, channels, chunk), chunk_rows(2 * f + 1, channels, chunk)
+            are, aim, bre, bim = left_ref[re, lanes], left_ref[im, lanes], right_ref[re, lanes], right_ref[im, lanes]
+            mre, mim = facet_model(degrid_ref, f, lanes, ramp)
             pre, pim = are * bre + aim * bim, aim * bre - are * bim
             vre, vim = pre * mre - pim * mim, pre * mim + pim * mre
             pred_re = vre if pred_re is None else pred_re + vre
             pred_im = vim if pred_im is None else pred_im + vim
-        ere = scale_ref[:, ln] * (pred_re - vis_ref[0, at, ln].astype(F32))
-        eim = scale_ref[:, ln] * (pred_im - vis_ref[1, at, ln].astype(F32))
+            products.append((pre, pim))
+        ere = scale_ref[:, lanes] * (pred_re - vis_ref[0, at, lanes].astype(F32))
+        eim = scale_ref[:, lanes] * (pred_im - vis_ref[1, at, lanes].astype(F32))
+        error_ref[0, at, lanes] = ere
+        error_ref[1, at, lanes] = eim
         for f in range(facets):
-            are, aim, bre, bim, mre, mim = parts(f)
-            qre, qim = ere * mre + eim * mim, eim * mre - ere * mim
-            values = (
-                (qre * bre - qim * bim, qre * bim + qim * bre),
-                (qre * are + qim * aim, qre * aim - qim * are),
-            )
-            for side in range(2):
-                for c in range(2):
-                    hi, lo = halves(values[side][c])
-                    first = 2 * side * rows + lanes * width
-                    grads_ref[rows_of(2 * f + c), first : first + width] = hi
-                    grads_ref[rows_of(2 * f + c), first + rows : first + rows + width] = lo
-            pre, pim = are * bre + aim * bim, aim * bre - are * bim
+            pre, pim = products[f]
             models = (ere * pre + eim * pim, eim * pre - ere * pim)
             for c in range(2):
                 n = c * facets + f
                 slope = models[c] * ramp
-                grad_degrid_ref[0, n, :, ln] += models[c][:8] + models[c][8:]
-                grad_degrid_ref[1, n, :, ln] += slope[:8] + slope[8:]
+                grad_degrid_ref[0, n, :, lanes] += models[c][:8] + models[c][8:]
+                grad_degrid_ref[1, n, :, lanes] += slope[:8] + slope[8:]
+
+
+def gain_step(f, chunk, channels, degrid_ref, left_ref, right_ref, error_ref, grads_ref, width=LANES):
+    rows = error_ref.shape[2]
+    at = chunk_rows(0, channels, chunk)
+    ramp = channel_ramp(channels, chunk, width)
+    re, im = chunk_rows(2 * f, channels, chunk), chunk_rows(2 * f + 1, channels, chunk)
+    for first in range(0, rows, width):
+        lanes = slice(first, first + width)
+        are, aim, bre, bim = left_ref[re, lanes], left_ref[im, lanes], right_ref[re, lanes], right_ref[im, lanes]
+        mre, mim = facet_model(degrid_ref, f, lanes, ramp)
+        ere, eim = error_ref[0, at, lanes], error_ref[1, at, lanes]
+        qre, qim = ere * mre + eim * mim, eim * mre - ere * mim
+        values = (
+            (qre * bre - qim * bim, qre * bim + qim * bre),
+            (qre * are + qim * aim, qre * aim - qim * are),
+        )
+        for side in range(2):
+            for c in range(2):
+                hi, lo = halves(values[side][c])
+                start = 2 * side * rows + first
+                grads_ref[chunk_rows(c, channels, chunk), start : start + width] = hi
+                grads_ref[chunk_rows(c, channels, chunk), start + rows : start + rows + width] = lo
 
 
 def place_grads(grad_degrid_ref, place_ref, store_value):
@@ -289,9 +307,9 @@
 def main_kernel(
     owner_ref, offset_ref, taps_ref, gain_ref, vis_ref, noise_ref, keep_ref, pairs_ref, sky_ref,
     words_ref, firsts_ref, grad_ref, data_ref,
-    send_a, mid_a, got_a, send_c, mid_c, got_c, send_e, mid_e, got_e, own, gains, send_g, got_g, near,
+    send_a, mid_a, got_a, send_c, mid_c, got_c, send_e, mid_e, got_e, own, gains, send_g, pair_g, sum_g, got_g, near,
     place, stage, cells, weight, product, slots, part, degrid, turned, gather, sums, scale,
-    left, right, grads, grad_degrid,
+    left, right, error, grads_even, grads_odd, grad_degrid,
     sky_sem, slot_sem, sem_a, sem_c, sem_e, gain_sem, pair_sem, near_sem, sum_sem,
     channels, times, groups,
 ):
@@ -365,6 +383,10 @@
     slot_copy = pltpu.make_async_copy(firsts_ref, slots, slot_sem)
     slot_copy.start()
     spread_taps(words_ref, weight)
+    column = gains.at[:, core]
+    pair = (time, group + 1 - 2 * core)
+    wait_bytes(column, gain_sem.at[1])
+    remote(column, column, pair_sem.at[0], pair_sem.at[1], pair).start()
     slot_copy.wait()
 
     def store_value(h, value):
@@ -372,22 +394,18 @@
 
     degrid_slots(slots, words_ref, cells, weight, product, store_value)
     second.start()
-
-    column = gains.at[:, core]
-    wait_bytes(column, gain_sem.at[1])
-    to_pair = remote(column, column, pair_sem.at[0], pair_sem.at[1], (time, group + 1 - 2 * core))
-    to_pair.start()
-    second.pass_on()
     wait_bytes(column, pair_sem.at[1])
     turn_gains(gains, turned, channels)
-    gather_gains(turned, gather, left, right)
+    gather_gains(turned, gather, left, right, 0, 2)
+    second.pass_on()
+    gather_gains(turned, gather, left, right, 2, 3)
 
     second.wait_receive()
     gather_degrid(lambda h: got_c[:, :, h, :].reshape(devices, LANES), place, part, degrid)
 
     @pl.loop(0, channels // CHUNK)
     def _(chunk):
-        row_step(chunk, channels, vis_ref, scale, degrid, left, right, grads, grad_degrid)
+        error_step(chunk, channels, vis_ref, scale, degrid, left, right, error, grad_degrid, 2 * LANES)
 
     def store_grad(h, value):
         send_e[:, :, h, :] = value.reshape(times, groups, LANES)
@@ -397,35 +415,55 @@
 
     batch = 4
 
-    def sum_batch(b):
-        for i in range(batch):
-            fc = b * batch + i
-            value = dot_nt(sums[...], grads[fc * channels : (fc + 1) * channels, :])
-            send_g[fc] = jnp.concatenate([value, jnp.zeros((64, 2 * LANES - channels), F32)], axis=1)
-        these = pl.ds(b * batch, batch)
-        to_end = got_g.at[group, these]
-        pltpu.make_async_copy(send_g.at[these, pl.ds(group * 8, 8)], to_end, sum_sem.at[1]).start()
-
-        @pl.loop(1, groups)
+    def these(b):
+        return pl.ds(b * batch, batch)
+
+    def combine(b):
+        wait_bytes(pair_g.at[these(b)], sum_sem.at[3 + b])
+        for fc in range(b * batch, (b + 1) * batch):
+            sum_g[:, fc] = send_g[core, fc] + pair_g[fc]
+        to_end = got_g.at[level, these(b)]
+        pltpu.make_async_copy(sum_g.at[level, these(b)], to_end, sum_sem.at[2]).start()
+
+        @pl.loop(1, groups // 2)
         def _(n):
-            to = lax.rem(group + n, groups)
-            remote(send_g.at[these, pl.ds(to * 8, 8)], to_end, sum_sem.at[0], sum_sem.at[1], (time, to)).start()
-
-    sum_batch(0)
-    third.pass_on()
-    for b in range(1, 2 * facets // batch):
-        sum_batch(b)
+            to = lax.rem(level + n, groups // 2)
+            remote(sum_g.at[to, these(b)], to_end, sum_sem.at[1], sum_sem.at[2], (time, 2 * to + core)).start()
+
+    for f in range(facets):
+        grads = grads_even if f % 2 == 0 else grads_odd
+
+        @pl.loop(0, channels // CHUNK, unroll=5)
+        def _(chunk):
+            gain_step(f, chunk, channels, degrid, left, right, error, grads, 2 * LANES)
+
+        for c in range(2):
+            value = dot_nt(sums[...], grads[c * channels : (c + 1) * channels, :])
+            value = jnp.concatenate([value, jnp.zeros((64, 2 * LANES - channels), F32)], axis=1)
+            value = value.reshape(groups // 2, 2, 8, 2 * LANES)
+            for k in range(2):
+                send_g[k, 2 * f + c] = value[:, k]
+        b = (2 * f + 1) // batch
+        if (2 * f + 2) % batch == 0:
+            remote(
+                send_g.at[1 - core, these(b)], pair_g.at[these(b)], sum_sem.at[0], sum_sem.at[3 + b], pair
+            ).start()
+            if b > 0:
+                combine(b - 1)
+            if b == 1:
+                third.pass_on()
+    combine(2 * facets // batch - 1)
 
     third.wait_receive()
     grad_ref[...] = got_e[...].reshape(devices, 2, LANES)
     below.wait()
     above.wait()
-    wait_bytes(got_g, sum_sem.at[1])
+    wait_bytes(got_g, sum_sem.at[2])
     for f in range(facets):
         for c in range(2):
             fc = 2 * f + c
             total = got_g[0, fc]
-            for n in range(1, groups):
+            for n in range(1, groups // 2):
                 total = total + got_g[n, fc]
             smooth = []
             for lt in range(2):
@@ -441,7 +479,8 @@
     third.wait_send()
     wait_bytes(gains.at[pl.ds(0, groups // 2 - 1), 0], gain_sem.at[0])
     wait_bytes(column, pair_sem.at[0])
-    wait_bytes(got_g.at[pl.ds(0, groups - 1)], sum_sem.at[0])
+    wait_bytes(pair_g, sum_sem.at[0])
+    wait_bytes(got_g.at[pl.ds(0, groups // 2 - 1)], sum_sem.at[1])
 
 
 def scatter_kernel(first_ref, words_ref, grad_ref, sky_ref, weight_ref, spread, cells, stage, sem):
@@ -536,8 +575,10 @@
             pairs, middle_pairs, pairs,
             pltpu.VMEM((8, tiles, LANES), F32),
             pltpu.VMEM((groups // 2, 2, 8, tiles, LANES), F32),
-            pltpu.VMEM((2 * facets, 64, 2 * LANES), F32),
-            pltpu.VMEM((groups, 2 * facets, 8, 2 * LANES), F32),
+            pltpu.VMEM((2, 2 * facets, groups // 2, 8, 2 * LANES), F32),
+            pltpu.VMEM((2 * facets, groups // 2, 8, 2 * LANES), F32),
+            pltpu.VMEM((groups // 2, 2 * facets, 8, 2 * LANES), F32),
+            pltpu.VMEM((groups // 2, 2 * facets, 8, 2 * LANES), F32),
             pltpu.VMEM((2, 8, tiles, LANES), F32),
             pltpu.VMEM((8, devices, rows), BF16),
             pltpu.VMEM(sky.shape, F32),
@@ -553,7 +594,9 @@
             pltpu.VMEM((1, rows), F32),
             pltpu.VMEM((2 * facets * channels, rows), F32),
             pltpu.VMEM((2 * facets * channels, rows), F32),
-            pltpu.VMEM((2 * facets * channels, 4 * rows), BF16),
+            pltpu.VMEM((2, channels, rows), F32),
+            pltpu.VMEM((2 * channels, 4 * rows), BF16),
+            pltpu.VMEM((2 * channels, 4 * rows), BF16),
             pltpu.VMEM((2, 2 * facets, 8, rows), F32),
             pltpu.SemaphoreType.DMA,
             pltpu.SemaphoreType.DMA,
@@ -563,7 +606,7 @@
             pltpu.SemaphoreType.DMA((2,)),
             pltpu.SemaphoreType.DMA((2,)),
             pltpu.SemaphoreType.DMA((4,)),
-            pltpu.SemaphoreType.DMA((2,)),
+            pltpu.SemaphoreType.DMA((7,)),
         ],
         compiler_params=pltpu.CompilerParams(
             vmem_limit_bytes=62 << 20, collective_id=0, has_side_effects=True

time: 72.3 us -> 67 us (0.927)
  Pallas kernels: 70.5 us -> 65.5 us
    pallas_call x1, Pallas kernels: 61.8 us -> 55.9 us  [body(): pl.pallas_call(functools.partial(main_kernel, channels=channels, times=ti...]
    pallas_call x1, Pallas kernels: 8.67 us -> 9.62 us  [body(): pl.pallas_call(scatter_kernel, out_shape=shape(sky.shape), in_specs=[pl.B...]
where the time goes in v4:
time: 67 us; the launch traced here: 66.8 us
  Pallas kernels  65.5 us (98%)
  between operations  0.67 us (1%)
    pallas_call x1, Pallas kernels, body(): pl.pallas_call(functools.partial(main_kernel, channels=channels, times=ti...  55.9 us
    pallas_call x1, Pallas kernels, body(): pl.pallas_call(scatter_kernel, out_shape=shape(sky.shape), in_specs=[pl.B...  9.62 us

profile of v4, /device:TPU:1, one launch (start us, length us, event | category | flops | bytes accessed | tf_op | source)
XLA Modules:
  0.0 66.8 jit_solution(8364031411980660684)
XLA Ops:
  0.6 55.9 %main.1 = (f32[128,128]{1,0:T(8,128)}, s32[8,128]{1,0:T(8,128)}, f32[128,2,128]{2,1,0:T(2,128)}, f32[8,8,2,240]{3,2,1,0:T(2,128)}) custom-call(s32[1,512]{1,0:T(1,128)} %bitcast.22, s32[1,512]{1,0:T(1,128)} %bitcast.23, f32[8,512]{1,0:T(8,128)} %taps_ref.1, f32[8,8,2,240]{3,2,1,0:T(2,128)} %bitcast.20, bf16[2,240,512]{2,1,0:T(8,128)(2,1)} %bitcast.19, ...), custom_call_target="tpu_custom_call" | custom-call | tf_op jit(solution)/shard_map/main/pallas_call | solution.py:562
  56.5 0.0 copy-start
  56.5 9.6 %scatter.1 = f32[16,512,128]{2,1,0:T(8,128)} custom-call(s32[8,128]{1,0:T(8,128)} %get-tuple-element.7.first_ref, f32[128,128]{1,0:T(8,128)} %get-tuple-element.8.words_ref, f32[128,2,128]{2,1,0:T(2,128)} %get-tuple-element.9.grad_ref), custom_call_target="tpu_custom_call" | custom-call | tf_op jit(solution)/shard_map/scatter/pallas_call | solution.py:621
  66.2 0.0 copy-done
  66.2 0.7 copy.14
Async XLA Ops:
  56.5 9.6 %copy-start = (f32[8,8,2,240]{3,2,1,0:T(2,128)S(1)}, f32[8,8,2,240]{3,2,1,0:T(2,128)}, u32[]{:S(2)}) copy-start(f32[8,8,2,240]{3,2,1,0:T(2,128)} %get-tuple-element.6) | copy-start | bytes 368644

commit v5 on v4

--- a/solution.py
+++ b/solution.py
@@ -1,4 +1,5 @@
 import functools
+import math
 
 import jax
 import jax.numpy as jnp
@@ -293,6 +294,50 @@
         wait_bytes(self.middle_ref.at[pl.ds(0, self.groups - 1)], self.sems.at[2])
 
 
+class DirectExchange:
+    def __init__(self, send_ref, middle_ref, receive_ref, sems, place, levels):
+        self.send_ref, self.middle_ref, self.receive_ref, self.sems = send_ref, middle_ref, receive_ref, sems
+        self.time, self.level, self.core = place
+        self.levels = levels
+
+    def start(self):
+        nodes, levels = self.send_ref.shape[0], self.levels
+        me = self.time * levels + self.level
+        to_middle = self.middle_ref.at[:, me]
+        pltpu.make_async_copy(self.send_ref.at[me], to_middle, self.sems.at[1]).start()
+
+        @pl.loop(0, nodes - 1)
+        def _(n):
+            to, level = far_first(n, self.time, self.level, nodes // levels, levels)
+            device = (to, 2 * level + self.core)
+            remote(self.send_ref.at[to * levels + level], to_middle, self.sems.at[0], self.sems.at[1], device).start()
+
+    def pass_on(self):
+        wait_bytes(self.middle_ref, self.sems.at[1])
+        to_end = self.receive_ref.at[self.core]
+        pltpu.make_async_copy(self.middle_ref.at[self.core], to_end, self.sems.at[3]).start()
+        pair = (self.time, 2 * self.level + 1 - self.core)
+        remote(self.middle_ref.at[1 - self.core], to_end, self.sems.at[2], self.sems.at[3], pair).start()
+
+    def wait_receive(self):
+        wait_bytes(self.receive_ref, self.sems.at[3])
+
+    def wait_send(self):
+        wait_bytes(self.send_ref.at[pl.ds(0, self.send_ref.shape[0] - 1)], self.sems.at[0])
+        wait_bytes(self.middle_ref.at[0], self.sems.at[2])
+
+
+def far_first(n, time, level, times, levels):
+    side = math.isqrt(times)
+
+    def offset(d):
+        return 2 + d - (d // 2) * (2 * d - 1)
+
+    x = lax.rem(time // side + offset(n // (side * levels)), side)
+    y = lax.rem(lax.rem(time, side) + offset(lax.rem(n // levels, side)), side)
+    return x * side + y, lax.rem(level + offset(lax.rem(n, levels)), levels)
+
+
 def remote(source, target, send_sem, receive_sem, device):
     return pltpu.make_async_remote_copy(
         src_ref=source, dst_ref=target, send_sem=send_sem, recv_sem=receive_sem,
@@ -307,7 +352,7 @@
 def main_kernel(
     owner_ref, offset_ref, taps_ref, gain_ref, vis_ref, noise_ref, keep_ref, pairs_ref, sky_ref,
     words_ref, firsts_ref, grad_ref, data_ref,
-    send_a, mid_a, got_a, send_c, mid_c, got_c, send_e, mid_e, got_e, own, gains, send_g, pair_g, sum_g, got_g, near,
+    send_a, mid_a, got_a, send_c, mid_c, got_c, send_e, mid_e, got_e, own, gains, send_g, pair_g, sum_g, got_g, near, prior,
     place, stage, cells, weight, product, slots, part, degrid, turned, gather, sums, scale,
     left, right, error, grads_even, grads_odd, grad_degrid,
     sky_sem, slot_sem, sem_a, sem_c, sem_e, gain_sem, pair_sem, near_sem, sum_sem,
@@ -319,28 +364,33 @@
     facets = gain_ref.shape[1]
     barrier = pltpu.get_barrier_semaphore()
 
-    @pl.loop(1, times)
+    levels = groups // 2
+    pair = (time, group + 1 - 2 * core)
+
+    def greet(device):
+        pl.semaphore_signal(barrier, inc=1, device_id=device, device_id_type=pl.DeviceIdType.MESH)
+
+    @pl.loop(0, times * levels - 1)
     def _(n):
-        to = (lax.rem(time + n, times), group)
-        pl.semaphore_signal(barrier, inc=1, device_id=to, device_id_type=pl.DeviceIdType.MESH)
-
-    @pl.loop(1, groups)
+        to, at = far_first(n, time, level, times, levels)
+        greet((to, 2 * at + core))
+
+    @pl.loop(0, levels)
     def _(n):
-        to = (time, lax.rem(group + n, groups))
-        pl.semaphore_signal(barrier, inc=1, device_id=to, device_id_type=pl.DeviceIdType.MESH)
+        greet((time, 2 * n + 1 - core))
 
     sky_copy = pltpu.make_async_copy(sky_ref, stage, sky_sem)
     sky_copy.start()
 
     def store_message(message):
         for t in range(devices):
-            send_a[t // groups, t % groups] = message[t : t + 1, :]
+            send_a[t // 2, t % 2] = message[t : t + 1, :]
 
     form_slots(owner_ref, offset_ref, taps_ref, place, store_message)
-    pl.semaphore_wait(barrier, times + groups - 2)
-
-    first = Exchange(send_a, mid_a, got_a, sem_a, time, group)
-    second = Exchange(send_c, mid_c, got_c, sem_c, time, group)
+    pl.semaphore_wait(barrier, times * levels - 1 + levels)
+
+    first = DirectExchange(send_a, mid_a, got_a, sem_a, (time, level, core), levels)
+    second = DirectExchange(send_c, mid_c, got_c, sem_c, (time, level, core), levels)
     third = Exchange(send_e, mid_e, got_e, sem_e, time, group)
     first.start()
 
@@ -376,7 +426,8 @@
     grad_degrid[...] = jnp.zeros_like(grad_degrid)
 
     first.wait_receive()
-    words_ref[...] = got_a[...].reshape(devices, LANES)
+    for c in range(2):
+        words_ref[pl.ds(c, devices // 2, stride=2), :] = got_a[c, :, 0, :]
     turned_words = words_ref[...].T
     firsts = jnp.concatenate([turned_words[j * WORDS + 8 : j * WORDS + 9, :] for j in range(8)], axis=0)
     firsts_ref[...] = jnp.clip(firsts.astype(I32), 0, cells.shape[0] - 8)
@@ -384,13 +435,12 @@
     slot_copy.start()
     spread_taps(words_ref, weight)
     column = gains.at[:, core]
-    pair = (time, group + 1 - 2 * core)
     wait_bytes(column, gain_sem.at[1])
     remote(column, column, pair_sem.at[0], pair_sem.at[1], pair).start()
     slot_copy.wait()
 
     def store_value(h, value):
-        send_c[:, :, h, :] = value.reshape(times, groups, LANES)
+        send_c[:, :, h, :] = value.reshape(devices // 2, 2, LANES)
 
     degrid_slots(slots, words_ref, cells, weight, product, store_value)
     second.start()
@@ -399,9 +449,24 @@
     gather_gains(turned, gather, left, right, 0, 2)
     second.pass_on()
     gather_gains(turned, gather, left, right, 2, 3)
+    below.wait()
+    above.wait()
+    for f in range(facets):
+        for c in range(2):
+            smooth = []
+            for lt in range(2):
+                n = 4 * f + 2 * c + lt
+                here = own[:, n, :]
+                down = jnp.where(time > 0, here - near[0, :, n, :], 0.0)
+                up = jnp.where(time < times - 1, near[1, :, n, :] - here, 0.0)
+                smooth.append(smoothness * (down - up))
+            prior[2 * f + c] = jnp.concatenate(smooth, axis=1)
 
     second.wait_receive()
-    gather_degrid(lambda h: got_c[:, :, h, :].reshape(devices, LANES), place, part, degrid)
+    for h in range(2):
+        for c in range(2):
+            part[h, pl.ds(c, devices // 2, stride=2), :] = got_c[c, :, h, :]
+    gather_degrid(lambda h: part[h], place, part, degrid)
 
     @pl.loop(0, channels // CHUNK)
     def _(chunk):
@@ -413,7 +478,7 @@
     place_grads(grad_degrid, place, store_grad)
     third.start()
 
-    batch = 4
+    batch = 2
 
     def these(b):
         return pl.ds(b * batch, batch)
@@ -450,28 +515,19 @@
             ).start()
             if b > 0:
                 combine(b - 1)
-            if b == 1:
+            if b == 3:
                 third.pass_on()
     combine(2 * facets // batch - 1)
 
     third.wait_receive()
     grad_ref[...] = got_e[...].reshape(devices, 2, LANES)
-    below.wait()
-    above.wait()
     wait_bytes(got_g, sum_sem.at[2])
     for f in range(facets):
         for c in range(2):
             fc = 2 * f + c
-            total = got_g[0, fc]
-            for n in range(1, groups // 2):
+            total = prior[fc]
+            for n in range(levels):
                 total = total + got_g[n, fc]
-            smooth = []
-            for lt in range(2):
-                here = own[:, 2 * fc + lt, :]
-                down = jnp.where(time > 0, here - near[0, :, 2 * fc + lt, :], 0.0)
-                up = jnp.where(time < times - 1, near[1, :, 2 * fc + lt, :] - here, 0.0)
-                smooth.append(down - up)
-            total = total + smoothness * jnp.concatenate(smooth, axis=1)
             data_ref[:, f, c, :] = total[:, :channels]
 
     first.wait_send()
@@ -498,7 +554,7 @@
             part = jnp.concatenate(halves(jnp.where(lane_quarter == g, block, 0.0)), axis=1)
             spread[j] = jnp.where(slot_quarter(words_ref, j) == lane_quarter.astype(F32), dot(part, fold), 0.0)
 
-    @pl.loop(0, sources, unroll=2)
+    @pl.loop(0, sources)
     def _(s):
         at = pl.ds(pl.multiple_of(s * 8, 8), 8)
         for j in range(8):
@@ -555,8 +611,7 @@
     sky = sky.reshape(parts * facets, lines * terms, LANES)
 
     times, groups = lax.axis_size("tm"), lax.axis_size("bl")
-    singles, pairs = pltpu.VMEM((times, groups, 1, LANES), F32), pltpu.VMEM((times, groups, 2, LANES), F32)
-    middle_singles = pltpu.VMEM((groups, times, 1, LANES), F32)
+    pairs = pltpu.VMEM((times, groups, 2, LANES), F32)
     middle_pairs = pltpu.VMEM((groups, times, 2, LANES), F32)
     tiles = facets * 4
     words, firsts, grad, data = pl.pallas_call(
@@ -570,9 +625,15 @@
         in_specs=vmem(8) + [pl.BlockSpec(memory_space=pl.ANY)],
         out_specs=tuple(vmem(4)),
         scratch_shapes=[
-            singles, middle_singles, singles,
-            pairs, middle_pairs, pairs,
-            pairs, middle_pairs, pairs,
+            pltpu.VMEM((devices // 2, 2, 1, LANES), F32),
+            pltpu.VMEM((2, devices // 2, 1, LANES), F32),
+            pltpu.VMEM((2, devices // 2, 1, LANES), F32),
+            pltpu.VMEM((devices // 2, 2, 2, LANES), F32),
+            pltpu.VMEM((2, devices // 2, 2, LANES), F32),
+            pltpu.VMEM((2, devices // 2, 2, LANES), F32),
+            pairs,
+            middle_pairs,
+            pairs,
             pltpu.VMEM((8, tiles, LANES), F32),
             pltpu.VMEM((groups // 2, 2, 8, tiles, LANES), F32),
             pltpu.VMEM((2, 2 * facets, groups // 2, 8, 2 * LANES), F32),
@@ -580,6 +641,7 @@
             pltpu.VMEM((groups // 2, 2 * facets, 8, 2 * LANES), F32),
             pltpu.VMEM((groups // 2, 2 * facets, 8, 2 * LANES), F32),
             pltpu.VMEM((2, 8, tiles, LANES), F32),
+            pltpu.VMEM((2 * facets, 8, 2 * LANES), F32),
             pltpu.VMEM((8, devices, rows), BF16),
             pltpu.VMEM(sky.shape, F32),
             pltpu.VMEM((cells // BLOCK * STRIDE, LANES), F32),
@@ -606,7 +668,7 @@
             pltpu.SemaphoreType.DMA((2,)),
             pltpu.SemaphoreType.DMA((2,)),
             pltpu.SemaphoreType.DMA((4,)),
-            pltpu.SemaphoreType.DMA((7,)),
+            pltpu.SemaphoreType.DMA((3 + facets,)),
         ],
         compiler_params=pltpu.CompilerParams(
             vmem_limit_bytes=62 << 20, collective_id=0, has_side_effects=True

time: 67 us -> 67.7 us (1.010)
  Pallas kernels: 65.5 us -> 66.2 us
where the time goes in v5:
time: 67.7 us; the launch traced here: 67.5 us
  Pallas kernels  66.2 us (98%)
    pallas_call x1, Pallas kernels, body(): pl.pallas_call(functools.partial(main_kernel, channels=channels, times=ti...  56.5 us
    pallas_call x1, Pallas kernels, body(): pl.pallas_call(scatter_kernel, out_shape=shape(sky.shape), in_specs=[pl.B...  9.69 us

profile of v5, /device:TPU:1, one launch (start us, length us, event | category | flops | bytes accessed | tf_op | source)
XLA Modules:
  0.0 67.5 jit_solution(4826470369481764590)
XLA Ops:
  0.6 56.5 %main.1 = (f32[128,128]{1,0:T(8,128)}, s32[8,128]{1,0:T(8,128)}, f32[128,2,128]{2,1,0:T(2,128)}, f32[8,8,2,240]{3,2,1,0:T(2,128)}) custom-call(s32[1,512]{1,0:T(1,128)} %bitcast.22, s32[1,512]{1,0:T(1,128)} %bitcast.23, f32[8,512]{1,0:T(8,128)} %taps_ref.1, f32[8,8,2,240]{3,2,1,0:T(2,128)} %bitcast.20, bf16[2,240,512]{2,1,0:T(8,128)(2,1)} %bitcast.19, ...), custom_call_target="tpu_custom_call" | custom-call | tf_op jit(solution)/shard_map/main/pallas_call | solution.py:617
  57.2 0.0 copy-start
  57.2 9.7 %scatter.1 = f32[16,512,128]{2,1,0:T(8,128)} custom-call(s32[8,128]{1,0:T(8,128)} %get-tuple-element.7.first_ref, f32[128,128]{1,0:T(8,128)} %get-tuple-element.8.words_ref, f32[128,2,128]{2,1,0:T(2,128)} %get-tuple-element.9.grad_ref), custom_call_target="tpu_custom_call" | custom-call | tf_op jit(solution)/shard_map/scatter/pallas_call | solution.py:683
  66.9 0.0 copy-done
  66.9 0.7 copy.14
Async XLA Ops:
  57.2 9.7 %copy-start = (f32[8,8,2,240]{3,2,1,0:T(2,128)S(1)}, f32[8,8,2,240]{3,2,1,0:T(2,128)}, u32[]{:S(2)}) copy-start(f32[8,8,2,240]{3,2,1,0:T(2,128)} %get-tuple-element.6) | copy-start | bytes 368644

commit v6 on v4

--- a/solution.py
+++ b/solution.py
@@ -37,6 +37,12 @@
 
 def ones_where(mask):
     return jnp.where(mask, 1.0, 0.0).astype(BF16)
+
+
+def place_product(place_ref, both):
+    slots, devices, rows = place_ref.shape
+    product = dot_nt(place_ref[...].reshape(slots * devices, rows), both)
+    return (product[:, :LANES] + product[:, LANES:]).reshape(slots, devices, LANES)
 
 
 def form_slots(owner_ref, offset_ref, taps_ref, place_ref, store_message):
@@ -49,13 +55,15 @@
     row = (offset >> 9) * STRIDE + (offset & (LANES - 1))
     tail = jnp.where(iota((WORDS - 8, rows), 0) == 0, row, (offset >> 7) & 3).astype(F32)
     words = jnp.concatenate([taps_ref[...], tail], axis=0)
-    hi, lo = halves(jnp.concatenate([words] * 8, axis=0))
+    both = jnp.concatenate(halves(jnp.concatenate([words] * 8, axis=0)), axis=0)
+    rank = jnp.where(hits, rank, -1.0)
+    for j in range(8):
+        place_ref[j] = ones_where(rank == float(j))
+    tall = place_product(place_ref, both)
     group = iota((devices, LANES), 1) // WORDS
     message = jnp.zeros((devices, LANES), F32)
     for j in range(8):
-        place = ones_where(jnp.where(hits, rank, -1.0) == float(j))
-        place_ref[j] = place
-        message = jnp.where(group == j, dot_nt(place, hi) + dot_nt(place, lo), message)
+        message = jnp.where(group == j, tall[j], message)
     store_message(message)
 
 
@@ -184,8 +192,18 @@
     return tuple(degrid_ref[0, n : n + 1, lanes] + degrid_ref[1, n : n + 1, lanes] * ramp for n in (f, g))
 
 
+def pair_step(chunk, channels, left_ref, right_ref, pair_ref, facets, width=LANES):
+    for f in range(facets):
+        re, im = chunk_rows(2 * f, channels, chunk), chunk_rows(2 * f + 1, channels, chunk)
+        for first in range(0, left_ref.shape[1], width):
+            lanes = slice(first, first + width)
+            are, aim, bre, bim = left_ref[re, lanes], left_ref[im, lanes], right_ref[re, lanes], right_ref[im, lanes]
+            pair_ref[re, lanes] = are * bre + aim * bim
+            pair_ref[im, lanes] = aim * bre - are * bim
+
+
 def error_step(
-    chunk, channels, vis_ref, scale_ref, degrid_ref, left_ref, right_ref, error_ref, grad_degrid_ref, width=LANES
+    chunk, channels, vis_ref, scale_ref, degrid_ref, pair_ref, error_ref, grad_degrid_ref, width=LANES
 ):
     rows = vis_ref.shape[2]
     facets = degrid_ref.shape[1] // 2
@@ -193,22 +211,21 @@
     ramp = channel_ramp(channels, chunk, width)
     for first in range(0, rows, width):
         lanes = slice(first, first + width)
-        products, pred_re, pred_im = [], None, None
+        pred_re = pred_im = None
         for f in range(facets):
             re, im = chunk_rows(2 * f, channels, chunk), chunk_rows(2 * f + 1, channels, chunk)
-            are, aim, bre, bim = left_ref[re, lanes], left_ref[im, lanes], right_ref[re, lanes], right_ref[im, lanes]
+            pre, pim = pair_ref[re, lanes], pair_ref[im, lanes]
             mre, mim = facet_model(degrid_ref, f, lanes, ramp)
-            pre, pim = are * bre + aim * bim, aim * bre - are * bim
             vre, vim = pre * mre - pim * mim, pre * mim + pim * mre
             pred_re = vre if pred_re is None else pred_re + vre
             pred_im = vim if pred_im is None else pred_im + vim
-            products.append((pre, pim))
         ere = scale_ref[:, lanes] * (pred_re - vis_ref[0, at, lanes].astype(F32))
         eim = scale_ref[:, lanes] * (pred_im - vis_ref[1, at, lanes].astype(F32))
         error_ref[0, at, lanes] = ere
         error_ref[1, at, lanes] = eim
         for f in range(facets):
-            pre, pim = products[f]
+            re, im = chunk_rows(2 * f, channels, chunk), chunk_rows(2 * f + 1, channels, chunk)
+            pre, pim = pair_ref[re, lanes], pair_ref[im, lanes]
             models = (ere * pre + eim * pim, eim * pre - ere * pim)
             for c in range(2):
                 n = c * facets + f
@@ -250,13 +267,12 @@
         level = jnp.sum(grad_degrid_ref[0, n], axis=0, keepdims=True)
         slope = jnp.sum(grad_degrid_ref[1, n], axis=0, keepdims=True)
         full.append(jnp.where(odd, slope, level))
-    hi, lo = halves(jnp.concatenate(full, axis=0))
+    tall = place_product(place_ref, jnp.concatenate(halves(jnp.concatenate(full, axis=0)), axis=0))
     group = (iota((devices, LANES), 1) >> 1) & 3
     for h in range(2):
-        value = jnp.zeros((devices, LANES), F32)
-        for g in range(4):
-            place = place_ref[4 * h + g]
-            value = jnp.where(group == g, dot_nt(place, hi) + dot_nt(place, lo), value)
+        value = tall[4 * h]
+        for g in range(1, 4):
+            value = jnp.where(group == g, tall[4 * h + g], value)
         store_value(h, value)
 
 
@@ -309,7 +325,7 @@
     words_ref, firsts_ref, grad_ref, data_ref,
     send_a, mid_a, got_a, send_c, mid_c, got_c, send_e, mid_e, got_e, own, gains, send_g, pair_g, sum_g, got_g, near,
     place, stage, cells, weight, product, slots, part, degrid, turned, gather, sums, scale,
-    left, right, error, grads_even, grads_odd, grad_degrid,
+    left, right, pairs, error, grads_even, grads_odd, grad_degrid,
     sky_sem, slot_sem, sem_a, sem_c, sem_e, gain_sem, pair_sem, near_sem, sum_sem,
     channels, times, groups,
 ):
@@ -400,12 +416,16 @@
     second.pass_on()
     gather_gains(turned, gather, left, right, 2, 3)
 
+    @pl.loop(0, channels // CHUNK)
+    def _(chunk):
+        pair_step(chunk, channels, left, right, pairs, facets, 2 * LANES)
+
     second.wait_receive()
     gather_degrid(lambda h: got_c[:, :, h, :].reshape(devices, LANES), place, part, degrid)
 
     @pl.loop(0, channels // CHUNK)
     def _(chunk):
-        error_step(chunk, channels, vis_ref, scale, degrid, left, right, error, grad_degrid, 2 * LANES)
+        error_step(chunk, channels, vis_ref, scale, degrid, pairs, error, grad_degrid, 2 * LANES)
 
     def store_grad(h, value):
         send_e[:, :, h, :] = value.reshape(times, groups, LANES)
@@ -413,53 +433,25 @@
     place_grads(grad_degrid, place, store_grad)
     third.start()
 
-    batch = 4
+    batch = 2
 
     def these(b):
         return pl.ds(b * batch, batch)
 
     def combine(b):
-        wait_bytes(pair_g.at[these(b)], sum_sem.at[3 + b])
+        wait_bytes(pair_g.at[these(b)], sum_sem.at[2 + b])
         for fc in range(b * batch, (b + 1) * batch):
             sum_g[:, fc] = send_g[core, fc] + pair_g[fc]
         to_end = got_g.at[level, these(b)]
-        pltpu.make_async_copy(sum_g.at[level, these(b)], to_end, sum_sem.at[2]).start()
+        pltpu.make_async_copy(sum_g.at[level, these(b)], to_end, sum_sem.at[2 + facets + b]).start()
 
         @pl.loop(1, groups // 2)
         def _(n):
             to = lax.rem(level + n, groups // 2)
-            remote(sum_g.at[to, these(b)], to_end, sum_sem.at[1], sum_sem.at[2], (time, 2 * to + core)).start()
-
-    for f in range(facets):
-        grads = grads_even if f % 2 == 0 else grads_odd
-
-        @pl.loop(0, channels // CHUNK, unroll=5)
-        def _(chunk):
-            gain_step(f, chunk, channels, degrid, left, right, error, grads, 2 * LANES)
-
-        for c in range(2):
-            value = dot_nt(sums[...], grads[c * channels : (c + 1) * channels, :])
-            value = jnp.concatenate([value, jnp.zeros((64, 2 * LANES - channels), F32)], axis=1)
-            value = value.reshape(groups // 2, 2, 8, 2 * LANES)
-            for k in range(2):
-                send_g[k, 2 * f + c] = value[:, k]
-        b = (2 * f + 1) // batch
-        if (2 * f + 2) % batch == 0:
-            remote(
-                send_g.at[1 - core, these(b)], pair_g.at[these(b)], sum_sem.at[0], sum_sem.at[3 + b], pair
-            ).start()
-            if b > 0:
-                combine(b - 1)
-            if b == 1:
-                third.pass_on()
-    combine(2 * facets // batch - 1)
-
-    third.wait_receive()
-    grad_ref[...] = got_e[...].reshape(devices, 2, LANES)
-    below.wait()
-    above.wait()
-    wait_bytes(got_g, sum_sem.at[2])
-    for f in range(facets):
+            remote(sum_g.at[to, these(b)], to_end, sum_sem.at[1], sum_sem.at[2 + facets + b], (time, 2 * to + core)).start()
+
+    def finish(f):
+        wait_bytes(got_g.at[:, these(f)], sum_sem.at[2 + facets + f])
         for c in range(2):
             fc = 2 * f + c
             total = got_g[0, fc]
@@ -473,6 +465,35 @@
                 smooth.append(down - up)
             total = total + smoothness * jnp.concatenate(smooth, axis=1)
             data_ref[:, f, c, :] = total[:, :channels]
+
+    below.wait()
+    above.wait()
+    for f in range(facets):
+        grads = grads_even if f % 2 == 0 else grads_odd
+
+        @pl.loop(0, channels // CHUNK, unroll=5)
+        def _(chunk):
+            gain_step(f, chunk, channels, degrid, left, right, error, grads, 2 * LANES)
+
+        for c in range(2):
+            value = dot_nt(sums[...], grads[c * channels : (c + 1) * channels, :])
+            value = jnp.concatenate([value, jnp.zeros((64, 2 * LANES - channels), F32)], axis=1)
+            value = value.reshape(groups // 2, 2, 8, 2 * LANES)
+            for k in range(2):
+                send_g[k, 2 * f + c] = value[:, k]
+        remote(send_g.at[1 - core, these(f)], pair_g.at[these(f)], sum_sem.at[0], sum_sem.at[2 + f], pair).start()
+        if f > 0:
+            combine(f - 1)
+        if f > 4:
+            finish(f - 5)
+        if f == 3:
+            third.pass_on()
+    combine(facets - 1)
+    for f in range(facets - 5, facets - 1):
+        finish(f)
+    third.wait_receive()
+    grad_ref[...] = got_e[...].reshape(devices, 2, LANES)
+    finish(facets - 1)
 
     first.wait_send()
     second.wait_send()
@@ -555,9 +576,9 @@
     sky = sky.reshape(parts * facets, lines * terms, LANES)
 
     times, groups = lax.axis_size("tm"), lax.axis_size("bl")
-    singles, pairs = pltpu.VMEM((times, groups, 1, LANES), F32), pltpu.VMEM((times, groups, 2, LANES), F32)
+    singles, doubles = pltpu.VMEM((times, groups, 1, LANES), F32), pltpu.VMEM((times, groups, 2, LANES), F32)
     middle_singles = pltpu.VMEM((groups, times, 1, LANES), F32)
-    middle_pairs = pltpu.VMEM((groups, times, 2, LANES), F32)
+    middle_doubles = pltpu.VMEM((groups, times, 2, LANES), F32)
     tiles = facets * 4
     words, firsts, grad, data = pl.pallas_call(
         functools.partial(
@@ -571,8 +592,8 @@
         out_specs=tuple(vmem(4)),
         scratch_shapes=[
             singles, middle_singles, singles,
-            pairs, middle_pairs, pairs,
-            pairs, middle_pairs, pairs,
+            doubles, middle_doubles, doubles,
+            doubles, middle_doubles, doubles,
             pltpu.VMEM((8, tiles, LANES), F32),
             pltpu.VMEM((groups // 2, 2, 8, tiles, LANES), F32),
             pltpu.VMEM((2, 2 * facets, groups // 2, 8, 2 * LANES), F32),
@@ -594,6 +615,7 @@
             pltpu.VMEM((1, rows), F32),
             pltpu.VMEM((2 * facets * channels, rows), F32),
             pltpu.VMEM((2 * facets * channels, rows), F32),
+            pltpu.VMEM((2 * facets * channels, rows), F32),
             pltpu.VMEM((2, channels, rows), F32),
             pltpu.VMEM((2 * channels, 4 * rows), BF16),
             pltpu.VMEM((2 * channels, 4 * rows), BF16),
@@ -606,7 +628,7 @@
             pltpu.SemaphoreType.DMA((2,)),
             pltpu.SemaphoreType.DMA((2,)),
             pltpu.SemaphoreType.DMA((4,)),
-            pltpu.SemaphoreType.DMA((7,)),
+            pltpu.SemaphoreType.DMA((2 + 2 * facets,)),
         ],
         compiler_params=pltpu.CompilerParams(
             vmem_limit_bytes=62 << 20, collective_id=0, has_side_effects=True

time: 67 us -> 65.8 us (0.982)
  Pallas kernels: 65.5 us -> 64.3 us
    pallas_call x1, Pallas kernels: 55.9 us -> 54.3 us  [body(): pl.pallas_call(functools.partial(main_kernel, channels=channels, times=ti...]
where the time goes in v6:
time: 65.8 us; the launch traced here: 65.7 us
  Pallas kernels  64.3 us (98%)
  between operations  0.67 us (1%)
  local copies, waits for them, and re-layouts  0.66 us (1%)
    pallas_call x1, Pallas kernels, body(): pl.pallas_call(functools.partial(main_kernel, channels=channels, times=ti...  54.3 us
    pallas_call x1, Pallas kernels, body(): pl.pallas_call(scatter_kernel, out_shape=shape(sky.shape), in_specs=[pl.B...  10 us

profile of v6, /device:TPU:1, one launch (start us, length us, event | category | flops | bytes accessed | tf_op | source)
XLA Modules:
  0.0 65.7 jit_solution(7965505763824902492)
XLA Ops:
  0.6 54.3 %main.1 = (f32[128,128]{1,0:T(8,128)}, s32[8,128]{1,0:T(8,128)}, f32[128,2,128]{2,1,0:T(2,128)}, f32[8,8,2,240]{3,2,1,0:T(2,128)}) custom-call(s32[1,512]{1,0:T(1,128)} %bitcast.22, s32[1,512]{1,0:T(1,128)} %bitcast.23, f32[8,512]{1,0:T(8,128)} %taps_ref.1, f32[8,8,2,240]{3,2,1,0:T(2,128)} %bitcast.20, bf16[2,240,512]{2,1,0:T(8,128)(2,1)} %bitcast.19, ...), custom_call_target="tpu_custom_call" | custom-call | tf_op jit(solution)/shard_map/main/pallas_call | solution.py:583
  55.0 0.0 copy-start
  55.0 10.0 %scatter.1 = f32[16,512,128]{2,1,0:T(8,128)} custom-call(s32[8,128]{1,0:T(8,128)} %get-tuple-element.7.first_ref, f32[128,128]{1,0:T(8,128)} %get-tuple-element.8.words_ref, f32[128,2,128]{2,1,0:T(2,128)} %get-tuple-element.9.grad_ref), custom_call_target="tpu_custom_call" | custom-call | tf_op jit(solution)/shard_map/scatter/pallas_call | solution.py:643
  65.0 0.0 copy-done
  65.0 0.7 %copy.14 = f32[1,8,8,2,240]{4,3,2,1,0:T(2,128)} copy(f32[1,8,8,2,240]{4,3,2,1,0:T(2,128)S(1)} %bitcast.21) | data formatting | bytes 245760
Async XLA Ops:
  55.0 10.0 %copy-start = (f32[8,8,2,240]{3,2,1,0:T(2,128)S(1)}, f32[8,8,2,240]{3,2,1,0:T(2,128)}, u32[]{:S(2)}) copy-start(f32[8,8,2,240]{3,2,1,0:T(2,128)} %get-tuple-element.6) | copy-start | bytes 368644

commit v7 on v6

--- a/solution.py
+++ b/solution.py
@@ -179,6 +179,8 @@
 
 
 def chunk_rows(plane, channels, chunk):
+    if isinstance(chunk, int):
+        return pl.ds(plane * channels + chunk * CHUNK, CHUNK)
     return pl.ds(pl.multiple_of(plane * channels + chunk * CHUNK, CHUNK), CHUNK)
 
 
@@ -423,7 +425,7 @@
     second.wait_receive()
     gather_degrid(lambda h: got_c[:, :, h, :].reshape(devices, LANES), place, part, degrid)
 
-    @pl.loop(0, channels // CHUNK)
+    @pl.loop(0, channels // CHUNK, unroll=3)
     def _(chunk):
         error_step(chunk, channels, vis_ref, scale, degrid, pairs, error, grad_degrid, 2 * LANES)
 
@@ -445,10 +447,11 @@
         to_end = got_g.at[level, these(b)]
         pltpu.make_async_copy(sum_g.at[level, these(b)], to_end, sum_sem.at[2 + facets + b]).start()
 
-        @pl.loop(1, groups // 2)
-        def _(n):
+        for n in range(1, groups // 2):
             to = lax.rem(level + n, groups // 2)
-            remote(sum_g.at[to, these(b)], to_end, sum_sem.at[1], sum_sem.at[2 + facets + b], (time, 2 * to + core)).start()
+            remote(
+                sum_g.at[to, these(b)], to_end, sum_sem.at[1], sum_sem.at[2 + facets + b], (time, 2 * to + core)
+            ).start()
 
     def finish(f):
         wait_bytes(got_g.at[:, these(f)], sum_sem.at[2 + facets + f])
@@ -468,28 +471,34 @@
 
     below.wait()
     above.wait()
-    for f in range(facets):
-        grads = grads_even if f % 2 == 0 else grads_odd
-
-        @pl.loop(0, channels // CHUNK, unroll=5)
-        def _(chunk):
-            gain_step(f, chunk, channels, degrid, left, right, error, grads, 2 * LANES)
-
+    def grads_of(f):
+        return grads_even if f % 2 == 0 else grads_odd
+
+    def sum_stations(f):
         for c in range(2):
-            value = dot_nt(sums[...], grads[c * channels : (c + 1) * channels, :])
+            value = dot_nt(sums[...], grads_of(f)[c * channels : (c + 1) * channels, :])
             value = jnp.concatenate([value, jnp.zeros((64, 2 * LANES - channels), F32)], axis=1)
             value = value.reshape(groups // 2, 2, 8, 2 * LANES)
             for k in range(2):
                 send_g[k, 2 * f + c] = value[:, k]
-        remote(send_g.at[1 - core, these(f)], pair_g.at[these(f)], sum_sem.at[0], sum_sem.at[2 + f], pair).start()
+
+    for f in range(facets + 1):
         if f > 0:
-            combine(f - 1)
-        if f > 4:
-            finish(f - 5)
-        if f == 3:
+            sum_stations(f - 1)
+        if f < facets:
+            for chunk in range(channels // CHUNK):
+                gain_step(f, chunk, channels, degrid, left, right, error, grads_of(f), 2 * LANES)
+        if f > 0:
+            b = f - 1
+            remote(send_g.at[1 - core, these(b)], pair_g.at[these(b)], sum_sem.at[0], sum_sem.at[2 + b], pair).start()
+        if f > 1:
+            combine(f - 2)
+        if f > 6:
+            finish(f - 7)
+        if f == 6:
             third.pass_on()
     combine(facets - 1)
-    for f in range(facets - 5, facets - 1):
+    for f in range(facets - 6, facets - 1):
         finish(f)
     third.wait_receive()
     grad_ref[...] = got_e[...].reshape(devices, 2, LANES)

time: 65.8 us -> 63.3 us (0.962)
  Pallas kernels: 64.3 us -> 61.9 us
    pallas_call x1, Pallas kernels: 10 us -> 8.7 us  [body(): pl.pallas_call(scatter_kernel, out_shape=shape(sky.shape), in_specs=[pl.B...]
    pallas_call x1, Pallas kernels: 54.3 us -> 53.2 us  [body(): pl.pallas_call(functools.partial(main_kernel, channels=channels, times=ti...]
where the time goes in v7:
time: 63.3 us; the launch traced here: 63.2 us
  Pallas kernels  61.9 us (98%)
  between operations  0.67 us (1%)
  local copies, waits for them, and re-layouts  0.66 us (1%)
    pallas_call x1, Pallas kernels, body(): pl.pallas_call(functools.partial(main_kernel, channels=channels, times=ti...  53.2 us
    pallas_call x1, Pallas kernels, body(): pl.pallas_call(scatter_kernel, out_shape=shape(sky.shape), in_specs=[pl.B...  8.7 us

profile of v7, /device:TPU:1, one launch (start us, length us, event | category | flops | bytes accessed | tf_op | source)
XLA Modules:
  0.0 63.2 jit_solution(9695219897751635319)
XLA Ops:
  0.6 53.2 %main.1 = (f32[128,128]{1,0:T(8,128)}, s32[8,128]{1,0:T(8,128)}, f32[128,2,128]{2,1,0:T(2,128)}, f32[8,8,2,240]{3,2,1,0:T(2,128)}) custom-call(s32[1,512]{1,0:T(1,128)} %bitcast.22, s32[1,512]{1,0:T(1,128)} %bitcast.23, f32[8,512]{1,0:T(8,128)} %taps_ref.1, f32[8,8,2,240]{3,2,1,0:T(2,128)} %bitcast.20, bf16[2,240,512]{2,1,0:T(8,128)(2,1)} %bitcast.19, ...), custom_call_target="tpu_custom_call" | custom-call | tf_op jit(solution)/shard_map/main/pallas_call | solution.py:592
  53.8 0.0 copy-start
  53.8 8.7 %scatter.1 = f32[16,512,128]{2,1,0:T(8,128)} custom-call(s32[8,128]{1,0:T(8,128)} %get-tuple-element.7.first_ref, f32[128,128]{1,0:T(8,128)} %get-tuple-element.8.words_ref, f32[128,2,128]{2,1,0:T(2,128)} %get-tuple-element.9.grad_ref), custom_call_target="tpu_custom_call" | custom-call | tf_op jit(solution)/shard_map/scatter/pallas_call | solution.py:652
  62.5 0.0 copy-done
  62.5 0.7 %copy.14 = f32[1,8,8,2,240]{4,3,2,1,0:T(2,128)} copy(f32[1,8,8,2,240]{4,3,2,1,0:T(2,128)S(1)} %bitcast.21) | data formatting | bytes 245760
Async XLA Ops:
  53.8 8.7 %copy-start = (f32[8,8,2,240]{3,2,1,0:T(2,128)S(1)}, f32[8,8,2,240]{3,2,1,0:T(2,128)}, u32[]{:S(2)}) copy-start(f32[8,8,2,240]{3,2,1,0:T(2,128)} %get-tuple-element.6) | copy-start | bytes 368644

commit v8 on v7

--- a/solution.py
+++ b/solution.py
@@ -108,7 +108,7 @@
 def degrid_slots(first_ref, words_ref, cells_ref, weight_ref, product_ref, store_value):
     sources = words_ref.shape[0]
 
-    @pl.loop(0, sources, unroll=2)
+    @pl.loop(0, sources, unroll=8)
     def _(s):
         at = pl.ds(pl.multiple_of(s * 8, 8), 8)
         for j in range(8):
@@ -495,7 +495,7 @@
             combine(f - 2)
         if f > 6:
             finish(f - 7)
-        if f == 6:
+        if f == 5:
             third.pass_on()
     combine(facets - 1)
     for f in range(facets - 6, facets - 1):
@@ -513,7 +513,11 @@
     wait_bytes(got_g.at[pl.ds(0, groups // 2 - 1)], sum_sem.at[1])
 
 
-def scatter_kernel(first_ref, words_ref, grad_ref, sky_ref, weight_ref, spread, cells, stage, sem):
+def scatter_kernel(
+    first_ref, words_ref, grad_ref, data_ref, sky_ref, data_out_ref, weight_ref, spread, cells, stage, sem, data_sem
+):
+    data_copy = pltpu.make_async_copy(data_ref, data_out_ref, data_sem)
+    data_copy.start()
     sources = grad_ref.shape[0]
     blocks = stage.shape[1] // 8
     for b in range(blocks):
@@ -528,7 +532,7 @@
             part = jnp.concatenate(halves(jnp.where(lane_quarter == g, block, 0.0)), axis=1)
             spread[j] = jnp.where(slot_quarter(words_ref, j) == lane_quarter.astype(F32), dot(part, fold), 0.0)
 
-    @pl.loop(0, sources, unroll=2)
+    @pl.loop(0, sources)
     def _(s):
         at = pl.ds(pl.multiple_of(s * 8, 8), 8)
         for j in range(8):
@@ -542,7 +546,7 @@
         cells[head, :] = cells[head, :] + jnp.where(quarter > 0, pltpu.roll(pads, 2, 1), last)
         last = pltpu.roll(pads, LANES - 6, 1)
 
-    pieces = 4
+    pieces = sem.shape[0]
     length = blocks // pieces
 
     def copy(n):
@@ -559,6 +563,7 @@
         copy(n).start()
     for n in range(pieces):
         copy(n).wait()
+    data_copy.wait()
 
 
 def vmem(count):
@@ -649,21 +654,22 @@
         station_pairs, sky,
     )
 
-    out_grid = pl.pallas_call(
+    out_grid, data = pl.pallas_call(
         scatter_kernel,
-        out_shape=shape(sky.shape),
-        in_specs=[pl.BlockSpec(memory_space=pltpu.SMEM)] + vmem(2),
-        out_specs=pl.BlockSpec(memory_space=pl.ANY),
+        out_shape=(shape(sky.shape), shape(data.shape)),
+        in_specs=[pl.BlockSpec(memory_space=pltpu.SMEM)] + vmem(2) + [pl.BlockSpec(memory_space=pl.ANY)],
+        out_specs=(pl.BlockSpec(memory_space=pl.ANY), pl.BlockSpec(memory_space=pl.ANY)),
         scratch_shapes=[
             pltpu.VMEM((8, devices * 8, LANES), F32),
             pltpu.VMEM((8, devices, LANES), F32),
             pltpu.VMEM((cells // BLOCK * STRIDE, LANES), F32),
             pltpu.VMEM(sky.shape, F32),
-            pltpu.SemaphoreType.DMA((4,)),
+            pltpu.SemaphoreType.DMA((8,)),
+            pltpu.SemaphoreType.DMA,
         ],
         compiler_params=params(),
         name="scatter",
-    )(firsts, words, grad)
+    )(firsts, words, grad, data)
     grid_gradient = out_grid.reshape(parts, facets, lines, terms, LANES).transpose(0, 1, 3, 2, 4)
     grid_gradient = grid_gradient.reshape(sky_grid.shape)
 

time: 63.3 us -> 62.7 us (level); the launches traced: 63.2 us -> 61.5 us
  Pallas kernels: 61.9 us -> 60.7 us
  local copies, waits for them, and re-layouts: 0.66 us -> 0 us
    pallas_call x1, Pallas kernels: 53.2 us -> 52.3 us  [body(): pl.pallas_call(functools.partial(main_kernel, channels=channels, times=ti...]
    unnamed x3 -> x0, local copies, waits for them, and re-layouts: 0.66 us -> none
where the time goes in v8:
time: 62.7 us; the launch traced here: 61.5 us
  Pallas kernels  60.7 us (97%)
  between operations  0.8 us (1%)
    pallas_call x1, Pallas kernels, body(): pl.pallas_call(functools.partial(main_kernel, channels=channels, times=ti...  52.3 us
    pallas_call x1, Pallas kernels, body(): pl.pallas_call(scatter_kernel, out_shape=(shape(sky.shape), shape(data.sh...  8.38 us

profile of v8, /device:TPU:1, one launch (start us, length us, event | category | flops | bytes accessed | tf_op | source)
XLA Modules:
  0.0 61.5 jit_solution(3733941924287010419)
XLA Ops:
  0.6 52.3 %main.1 = (f32[128,128]{1,0:T(8,128)}, s32[8,128]{1,0:T(8,128)}, f32[128,2,128]{2,1,0:T(2,128)}, f32[8,8,2,240]{3,2,1,0:T(2,128)}) custom-call(s32[1,512]{1,0:T(1,128)} %bitcast.20, s32[1,512]{1,0:T(1,128)} %bitcast.21, f32[8,512]{1,0:T(8,128)} %taps_ref.1, f32[8,8,2,240]{3,2,1,0:T(2,128)} %bitcast.19, bf16[2,240,512]{2,1,0:T(8,128)(2,1)} %bitcast.18, ...), custom_call_target="tpu_custom_call" | custom-call | tf_op jit(solution)/shard_map/main/pallas_call | solution.py:597
  53.0 8.4 %scatter.1 = (f32[16,512,128]{2,1,0:T(8,128)}, f32[8,8,2,240]{3,2,1,0:T(2,128)}) custom-call(s32[8,128]{1,0:T(8,128)} %get-tuple-element.8.first_ref, f32[128,128]{1,0:T(8,128)} %get-tuple-element.9.words_ref, f32[128,2,128]{2,1,0:T(2,128)} %get-tuple-element.10.grad_ref, f32[8,8,2,240]{3,2,1,0:T(2,128)} %get-tuple-element.11.data_ref), custom_call_target="tpu_custom_call" | custom-call | tf_op jit(solution)/shard_map/scatter/pallas_call | solution.py:657

commit v9 on v8

--- a/solution.py
+++ b/solution.py
@@ -378,14 +378,6 @@
         to = lax.rem(group + 2 * n, groups)
         remote(own, mine, gain_sem.at[0], gain_sem.at[1], (time, to)).start()
 
-    def next_interval(n, step):
-        to = lax.rem(time + step, times)
-        return remote(own, near.at[n], near_sem.at[2 * n], near_sem.at[2 * n + 1], (to, group))
-
-    below, above = next_interval(0, 1), next_interval(1, times - 1)
-    below.start()
-    above.start()
-
     sky_copy.wait()
     transpose_grid(stage, cells)
     first.pass_on()
@@ -416,6 +408,13 @@
     turn_gains(gains, turned, channels)
     gather_gains(turned, gather, left, right, 0, 2)
     second.pass_on()
+    def next_interval(n, step):
+        to = lax.rem(time + step, times)
+        return remote(own, near.at[n], near_sem.at[2 * n], near_sem.at[2 * n + 1], (to, group))
+
+    below, above = next_interval(0, 1), next_interval(1, times - 1)
+    below.start()
+    above.start()
     gather_gains(turned, gather, left, right, 2, 3)
 
     @pl.loop(0, channels // CHUNK)

time: 62.7 us -> 62.9 us (level); the launches traced: 61.5 us -> 63 us
  Pallas kernels: 60.7 us -> 62.2 us
    pallas_call x1, Pallas kernels: 8.38 us -> 9.98 us  [body(): pl.pallas_call(scatter_kernel, out_shape=(shape(sky.shape), shape(data.sh...]
where the time goes in v9:
time: 62.9 us; the launch traced here: 63 us
  Pallas kernels  62.2 us (99%)
  between operations  0.8 us (1%)
    pallas_call x1, Pallas kernels, body(): pl.pallas_call(functools.partial(main_kernel, channels=channels, times=ti...  52.2 us
    pallas_call x1, Pallas kernels, body(): pl.pallas_call(scatter_kernel, out_shape=(shape(sky.shape), shape(data.sh...  9.98 us

profile of v9, /device:TPU:1, one launch (start us, length us, event | category | flops | bytes accessed | tf_op | source)
XLA Modules:
  0.0 63.0 jit_solution(4201586263958569926)
XLA Ops:
  0.6 52.2 %main.1 = (f32[128,128]{1,0:T(8,128)}, s32[8,128]{1,0:T(8,128)}, f32[128,2,128]{2,1,0:T(2,128)}, f32[8,8,2,240]{3,2,1,0:T(2,128)}) custom-call(s32[1,512]{1,0:T(1,128)} %bitcast.20, s32[1,512]{1,0:T(1,128)} %bitcast.21, f32[8,512]{1,0:T(8,128)} %taps_ref.1, f32[8,8,2,240]{3,2,1,0:T(2,128)} %bitcast.19, bf16[2,240,512]{2,1,0:T(8,128)(2,1)} %bitcast.18, ...), custom_call_target="tpu_custom_call" | custom-call | tf_op jit(solution)/shard_map/main/pallas_call | solution.py:596
  52.9 10.0 %scatter.1 = (f32[16,512,128]{2,1,0:T(8,128)}, f32[8,8,2,240]{3,2,1,0:T(2,128)}) custom-call(s32[8,128]{1,0:T(8,128)} %get-tuple-element.8.first_ref, f32[128,128]{1,0:T(8,128)} %get-tuple-element.9.words_ref, f32[128,2,128]{2,1,0:T(2,128)} %get-tuple-element.10.grad_ref, f32[8,8,2,240]{3,2,1,0:T(2,128)} %get-tuple-element.11.data_ref), custom_call_target="tpu_custom_call" | custom-call | tf_op jit(solution)/shard_map/scatter/pallas_call | solution.py:656
